TPU v7x, 128 devices: a whole 4x4x4 slice. The times are simulated.
128 devices in a mesh: row: 16 (over y_hi, x, core), blk: 2 (over y_lo), grp: 4 (over z).
Axes of the slice: x: 4, y: 4 (y_hi: 2, y_lo: 2; y = y_hi * 2 + y_lo), z: 4, core: 2. Of those that a mesh axis runs over, the one named last changes fastest.
Arguments:
- column_slab: bfloat16 [16384, 8192], P('row', ('blk', 'grp')), may hold values from -36 to 36
Outputs:
- rotated_slab: bfloat16 [16384, 8192], P('row', ('blk', 'grp'))
All inputs are finite; a program needn't handle non-finite values.
Results may differ from a plain program's by a relative error of at most 0.0049.
Values may be sent and summed in bfloat16 or wider, within the bound.
No kernel may reach another device: no remote copies, remote signals or barrier semaphores. Data moves between devices by JAX's collectives and lax.ppermute only.
A program may use at most 320 MiB of HBM per device.

v0:
```python
import jax
import jax.numpy as jnp
from jax import lax
from jax.sharding import PartitionSpec as P

B = 256
INNER = 2


def passed_along(array, axis, by):
    count = lax.axis_size(axis)
    pairs = [(i, i + by) for i in range(count) if 0 <= i + by < count]
    return lax.ppermute(array, axis, pairs)


def batched_dot(left_side, right_side):
    return jnp.einsum("pij,pjk->pik", left_side, right_side, precision=lax.Precision.HIGHEST)


def flipped(matrix):
    return jnp.swapaxes(matrix, 1, 2)


def cayley(current):
    half = current.shape[-1] // 2
    upper_block = current[:, :half, :half]
    lower_block = current[:, half:, half:]
    cross_block = current[:, :half, half:]
    diagonal_entries = jnp.diagonal(current, axis1=1, axis2=2)
    diag_mean = jnp.mean(diagonal_entries, axis=1) + 1e-06
    gradient = batched_dot(upper_block, cross_block) - batched_dot(cross_block, lower_block)
    coupling = -gradient / (diag_mean * diag_mean)[:, None, None]
    identity = jnp.broadcast_to(jnp.eye(half, dtype=jnp.float32), coupling.shape)
    outer_left = batched_dot(coupling, flipped(coupling))
    outer_right = batched_dot(flipped(coupling), coupling)
    factor_left = jnp.linalg.cholesky(identity + outer_left)
    factor_right = jnp.linalg.cholesky(identity + outer_right)
    left_part = jax.scipy.linalg.cho_solve(
        (factor_left, True), jnp.concatenate([identity - outer_left, -2.0 * coupling], axis=2)
    )
    right_part = jax.scipy.linalg.cho_solve(
        (factor_right, True),
        jnp.concatenate([2.0 * flipped(coupling), identity - outer_right], axis=2),
    )
    return flipped(jnp.concatenate([left_part, right_part], axis=1))


def rotation(gram_blocks):
    current = gram_blocks
    accumulated = None
    for sweep_index in range(INNER):
        rotor = cayley(current)
        accumulated = rotor if sweep_index == 0 else batched_dot(accumulated, rotor)
        if sweep_index + 1 < INNER:
            current = batched_dot(flipped(rotor), batched_dot(current, rotor))
    return accumulated.astype(jnp.bfloat16)


def body(column_slab):
    local_rows, local_cols = column_slab.shape
    pair_width = 2 * B
    pair_count = local_cols // pair_width
    chain_size = lax.axis_size(("blk", "grp"))
    position = lax.axis_index(("blk", "grp"))
    slot_index = jnp.arange(pair_count)[None, :, None]
    first_device = position == 0
    last_device = position == chain_size - 1
    pair_cols = column_slab.reshape(local_rows, pair_count, pair_width)
    gram_local = jnp.einsum(
        "rpa,rpb->pab", pair_cols, pair_cols, preferred_element_type=jnp.float32
    )
    gram_blocks = lax.psum(gram_local, "row")
    rotors = rotation(gram_blocks)
    pair_cols = jnp.einsum(
        "rpa,pab->rpb", pair_cols, rotors, preferred_element_type=jnp.float32
    ).astype(jnp.bfloat16)
    upper_half = pair_cols[:, :, :B]
    lower_half = pair_cols[:, :, B:]
    from_before = passed_along(upper_half[:, pair_count - 1, :], ("blk", "grp"), 1)
    from_after = passed_along(lower_half[:, 0, :], ("blk", "grp"), -1)
    shifted_upper = jnp.concatenate([from_before[:, None, :], upper_half[:, :-1, :]], axis=1)
    shifted_upper = jnp.where(first_device & (slot_index == 0), upper_half, shifted_upper)
    shifted_upper = jnp.where(first_device & (slot_index == 1), lower_half[:, :1, :], shifted_upper)
    shifted_lower = jnp.concatenate([lower_half[:, 1:, :], from_after[:, None, :]], axis=1)
    shifted_lower = jnp.where(
        last_device & (slot_index == pair_count - 1), upper_half[:, -1:, :], shifted_lower
    )
    pair_cols = jnp.concatenate([shifted_upper, shifted_lower], axis=2)
    return pair_cols.reshape(local_rows, local_cols)


def solution(mesh):
    return jax.shard_map(
        body,
        mesh=mesh,
        in_specs=(P("row", ("blk", "grp")),),
        out_specs=P("row", ("blk", "grp")),
        check_vma=False,
    )
```

profile of v0, /device:TPU:8, one launch (start us, length us, event | category | flops | bytes accessed | tf_op | source)
XLA Modules:
  0.0 868.6 jit_solution(12242182320586447517)
XLA Ops:
  14.2 143.5 %all-reduce.3.cloned.1.call-done = f32[2,512,512]{2,1,0:T(8,128)} async-done(((f32[2,512,512]{2,1,0:T(8,128)}), f32[2,512,512]{2,1,0:T(8,128)}) %all-reduce.3.cloned.1.call-update) | async-done | bytes 2097168 | tf_op jit(solution)/shard_map/psum | solution.py:72
  157.7 60.2 %copy.72 = f32[2,512,512]{0,2,1:T(8,128)} copy(f32[2,512,512]{2,1,0:T(8,128)} %all-reduce.3.cloned.1.call-done) | data formatting | bytes 4194304 | tf_op jit(solution)/shard_map/psum | solution.py:72
  217.9 5.5 gather_fusion
  236.1 23.5 %custom-call.31 = f32[2,128,128]{2,1,0:T(8,128)S(1)} custom-call(f32[2,128,128]{2,1,0:T(8,128)S(1)} %cholesky.350), custom_call_target="Cholesky" | custom-call | tf_op jit(solution)/shard_map/jit(cholesky)/cholesky | solution.py:36
  260.5 23.6 %custom-call.35 = f32[2,128,128]{2,1,0:T(8,128)S(1)} custom-call(f32[2,128,128]{2,1,0:T(8,128)S(1)} %cholesky.353), custom_call_target="Cholesky" | custom-call | tf_op jit(solution)/shard_map/jit(cholesky)/cholesky | solution.py:37
  285.5 20.3 %custom-call.36 = f32[2,1,128,128]{2,3,1,0:T(8,128)} custom-call(f32[2,1,128,128]{3,2,1,0:T(8,128)S(1)} %get-tuple-element.110), custom_call_target="InvertDiagBlocksLowerTriangular" | custom-call | tf_op jit(solution)/shard_map/jit(cholesky)/cholesky | solution.py:37
  310.0 24.9 %custom-call.37 = f32[2,128,128]{2,1,0:T(8,128)} custom-call(f32[2,128,128]{2,1,0:T(8,128)} %convolution_subtract_fusion.12), custom_call_target="Cholesky" | custom-call | tf_op jit(solution)/shard_map/jit(cholesky)/cholesky | solution.py:37
  334.8 21.5 %custom-call.32 = f32[2,1,128,128]{2,3,1,0:T(8,128)} custom-call(f32[2,1,128,128]{3,2,1,0:T(8,128)} %get-tuple-element.109), custom_call_target="InvertDiagBlocksLowerTriangular" | custom-call | tf_op jit(solution)/shard_map/jit(cholesky)/cholesky | solution.py:36
  361.0 24.9 %custom-call.33 = f32[2,128,128]{2,1,0:T(8,128)} custom-call(f32[2,128,128]{2,1,0:T(8,128)} %convolution_subtract_fusion.13), custom_call_target="Cholesky" | custom-call | tf_op jit(solution)/shard_map/jit(cholesky)/cholesky | solution.py:36
  396.8 40.7 %custom-call.34 = f32[2,2,128,128]{2,3,1,0:T(8,128)} custom-call(f32[2,2,128,128]{3,2,1,0:T(8,128)} %bitcast.201), custom_call_target="InvertDiagBlocksLowerTriangular" | custom-call | tf_op jit(solution)/shard_map/jit(_cho_solve)/vmap()/triangular_solve | solution.py:38
  444.8 7.2 while.9
  452.1 40.9 %custom-call.38 = f32[2,2,128,128]{2,3,1,0:T(8,128)} custom-call(f32[2,2,128,128]{3,2,1,0:T(8,128)} %bitcast.202), custom_call_target="InvertDiagBlocksLowerTriangular" | custom-call | tf_op jit(solution)/shard_map/jit(_cho_solve)/vmap()/triangular_solve | solution.py:41
  507.5 59.5 %copy.93 = f32[2,512,512]{0,2,1:T(8,128)} copy(f32[2,512,512]{2,1,0:T(8,128)S(1)} %fusion.50) | data formatting | bytes 4194304 | tf_op jit(solution)/shard_map/pij,pjk->pik/dot_general | solution.py:17
  568.4 5.7 gather_fusion.1
  580.7 23.5 %custom-call.43 = f32[2,128,128]{2,1,0:T(8,128)S(1)} custom-call(f32[2,128,128]{2,1,0:T(8,128)S(1)} %cholesky.359), custom_call_target="Cholesky" | custom-call | tf_op jit(solution)/shard_map/jit(cholesky)/cholesky | solution.py:37
  604.5 23.5 %custom-call.39 = f32[2,128,128]{2,1,0:T(8,128)S(1)} custom-call(f32[2,128,128]{2,1,0:T(8,128)S(1)} %cholesky.356), custom_call_target="Cholesky" | custom-call | tf_op jit(solution)/shard_map/jit(cholesky)/cholesky | solution.py:36
  628.1 20.1 %custom-call.44 = f32[2,1,128,128]{2,3,1,0:T(8,128)S(1)} custom-call(f32[2,1,128,128]{3,2,1,0:T(8,128)S(1)} %get-tuple-element.108), custom_call_target="InvertDiagBlocksLowerTriangular" | custom-call | tf_op jit(solution)/shard_map/jit(cholesky)/cholesky | solution.py:37
  650.6 24.1 %custom-call.45 = f32[2,128,128]{2,1,0:T(8,128)} custom-call(f32[2,128,128]{2,1,0:T(8,128)S(1)} %convolution_subtract_fusion.10), custom_call_target="Cholesky" | custom-call | tf_op jit(solution)/shard_map/jit(cholesky)/cholesky | solution.py:37
  674.7 20.3 %custom-call.40 = f32[2,1,128,128]{2,3,1,0:T(8,128)} custom-call(f32[2,1,128,128]{3,2,1,0:T(8,128)S(1)} %get-tuple-element.107), custom_call_target="InvertDiagBlocksLowerTriangular" | custom-call | tf_op jit(solution)/shard_map/jit(cholesky)/cholesky | solution.py:36
  697.2 24.4 %custom-call.41 = f32[2,128,128]{2,1,0:T(8,128)S(1)} custom-call(f32[2,128,128]{2,1,0:T(8,128)} %convolution_subtract_fusion.11), custom_call_target="Cholesky" | custom-call | tf_op jit(solution)/shard_map/jit(cholesky)/cholesky | solution.py:36
  731.2 40.7 %custom-call.42 = f32[2,2,128,128]{2,3,1,0:T(8,128)} custom-call(f32[2,2,128,128]{3,2,1,0:T(8,128)} %bitcast.203), custom_call_target="InvertDiagBlocksLowerTriangular" | custom-call | tf_op jit(solution)/shard_map/jit(_cho_solve)/vmap()/triangular_solve | solution.py:38
  781.4 39.5 %custom-call.46 = f32[2,2,128,128]{2,3,1,0:T(8,128)S(1)} custom-call(f32[2,2,128,128]{3,2,1,0:T(8,128)S(1)} %bitcast.200), custom_call_target="InvertDiagBlocksLowerTriangular" | custom-call | tf_op jit(solution)/shard_map/jit(_cho_solve)/vmap()/triangular_solve | solution.py:41
  825.2 6.9 fusion.16
  842.1 8.9 %collective-permute-done.1 = bf16[1024,256]{0,1:T(8,128)(2,1)} collective-permute-done((bf16[1024,256]{0,1:T(8,128)(2,1)S(1)}, bf16[1024,256]{0,1:T(8,128)(2,1)}, u32[]{:S(2)}, u32[]{:S(2)}) %collective-permute-start.1) | collective-permute-done | bytes 524320 | tf_op jit(solution)/shard_map/ppermute | solution.py:13
  (189 shorter events, 142.2 us)
Async XLA Ops:
  6.5 151.2 %all-reduce.3.cloned.1.call-start = ((), (), s32[]{:S(2)}) async-start(), calls=%async_computation | async-start | bytes 4194304 | tf_op jit(solution)/shard_map/psum | solution.py:72
  157.7 65.9 %copy-start = (f32[2,512,512]{2,1,0:T(8,128)S(1)}, f32[2,512,512]{2,1,0:T(8,128)}, u32[]{:S(2)}) copy-start(f32[2,512,512]{2,1,0:T(8,128)} %all-reduce.3.cloned.1.call-done) | copy-start | bytes 6291460
  228.8 4.2 copy-start.9
  284.1 1.4 copy-start.17
  437.6 2.1 copy-start.18
  442.7 50.3 %copy-start.8 = (f32[2,256,256]{1,2,0:T(8,128)S(1)}, f32[2,256,256]{1,2,0:T(8,128)}, u32[]{:S(2)}) copy-start(f32[2,256,256]{1,2,0:T(8,128)} %get-tuple-element.92) | copy-start | bytes 1572868
  493.0 3.8 copy-start.20
  497.4 2.9 copy-start.3
  498.0 5.9 copy-start.1
  500.4 3.6 copy-start.5
  580.7 47.3 %copy-start.24 = (pred[128,128]{1,0:T(8,128)(4,1)S(1)}, pred[128,128]{1,0:T(8,128)(4,1)}, u32[]{:S(2)}) copy-start(pred[128,128]{1,0:T(8,128)(4,1)} %iota_compare_fusion.2) | copy-start | bytes 49156
  604.5 117.2 %copy-start.23 = (pred[128,128]{1,0:T(8,128)(4,1)S(1)}, pred[128,128]{1,0:T(8,128)(4,1)}, u32[]{:S(2)}) copy-start(pred[128,128]{1,0:T(8,128)(4,1)} %iota_compare_fusion.3) | copy-start | bytes 49156
  628.0 95.6 %copy-start.21 = (pred[256,256]{1,0:T(8,128)(4,1)S(1)}, pred[256,256]{1,0:T(8,128)(4,1)}, u32[]{:S(2)}) copy-start(pred[256,256]{1,0:T(8,128)(4,1)} %iota_compare_fusion) | copy-start | bytes 196612
  722.7 49.3 %copy-start.10 = (f32[256,256]{1,0:T(8,128)S(1)}, f32[256,256]{1,0:T(8,128)}, u32[]{:S(2)}) copy-start(f32[256,256]{1,0:T(8,128)} %copy.166) | copy-start | bytes 786436
  722.7 49.2 %copy-start.11 = (f32[2,256,256]{2,1,0:T(8,128)S(1)}, f32[2,256,256]{2,1,0:T(8,128)}, u32[]{:S(2)}) copy-start(f32[2,256,256]{2,1,0:T(8,128)} %copy.99) | copy-start | bytes 1572868
  772.0 2.2 copy-start.19
  775.4 45.6 %copy-start.7 = (f32[2,256,256]{1,2,0:T(8,128)S(1)}, f32[2,256,256]{1,2,0:T(8,128)}, u32[]{:S(2)}) copy-start(f32[2,256,256]{1,2,0:T(8,128)} %get-tuple-element.90) | copy-start | bytes 1572868
  823.3 1.9 copy-start.2
  823.3 1.9 copy-start.4
  823.3 1.9 copy-start.6
  823.3 1.9 copy-start.22
  825.2 6.9 copy-start.25
  834.8 16.2 %collective-permute-start.1 = (bf16[1024,256]{0,1:T(8,128)(2,1)S(1)}, bf16[1024,256]{0,1:T(8,128)(2,1)}, u32[]{:S(2)}, u32[]{:S(2)}) collective-permute-start(bf16[1024,256]{0,1:T(8,128)(2,1)S(1)} %get-tuple-element.88), channel_id=1, source_target_pairs={{1,0},{2,1},{3,2},{4,3},{5,4},{6,5},{7,6},{9,8},{10,9},{11,10},{12... | collective-permute-start | bytes 1572872 | tf_op jit(solution)/shard_map/ppermute | solution.py:13
  840.1 17.4 %collective-permute-start = (bf16[1024,256]{0,1:T(8,128)(2,1)}, bf16[1024,256]{0,1:T(8,128)(2,1)}, u32[]{:S(2)}, u32[]{:S(2)}) collective-permute-start(bf16[1024,256]{0,1:T(8,128)(2,1)} %get-tuple-element.87), channel_id=1, source_target_pairs={{0,1},{1,2},{2,3},{3,4},{4,5},{5,6},{6,7},{8,9},{9,10},{10,11},{11... | collective-permute-start | bytes 1572872 | tf_op jit(solution)/shard_map/ppermute | solution.py:13
  (5 other events, 4.2 us)
Sparse Core Ops, SparseCore 0:
  11.5 146.1 all-reduce.2
where the time goes:
time: 879 us; the launch traced here: 869 us
  other arithmetic  455 us (52%)
  local copies, waits for them, and re-layouts  171 us (19%)
  waiting for transfers between devices  157 us (18%)
  matrix products  63.2 us (7%)
  between operations  14.4 us (2%)
    another operation x18, other arithmetic, cayley(): factor_left = jnp.linalg.cholesky(identity + outer_left)  144 us
    psum x1, waiting for transfers between devices, body(): gram_blocks = lax.psum(gram_local, 'row')  144 us
    another operation x12, other arithmetic, cayley(): factor_right = jnp.linalg.cholesky(identity + outer_right)  137 us
    another operation x6, other arithmetic, cayley(): jax.scipy.linalg.cho_solve((factor_left, True), jnp.concatenate([identity...  85.8 us
    another operation x2, other arithmetic, cayley(): jax.scipy.linalg.cho_solve((factor_right, True), jnp.concatenate([2.0 * f...  80.4 us
    dot_general x3, local copies, waits for them, and re-layouts, batched_dot(): jnp.einsum('pij,pjk->pik', left_side, right_side, precision=lax.Precision...  61.5 us
    psum x1, local copies, waits for them, and re-layouts, body(): gram_blocks = lax.psum(gram_local, 'row')  60.2 us
    dot_general x11, matrix products, batched_dot(): jnp.einsum('pij,pjk->pik', left_side, right_side, precision=lax.Precision...  24 us
  transfers between devices with their start and end apart: 3, of which 3 were waited for; matrix products, arithmetic and copies ran while one was open for 0% of the time, Pallas kernels for 0%

commit v1 on v0

v1 whole, which is shorter than its diff:
```python
import jax
import jax.numpy as jnp
from jax import lax
from jax.experimental import pallas as pl
from jax.experimental.pallas import tpu as pltpu
from jax.sharding import Mesh, PartitionSpec as P

B = 256
PAIR = 2 * B
INNER = 2
T = 128
BLOCKS = ((0, 0), (0, 1), (1, 1), (0, 2), (0, 3), (1, 2), (1, 3), (2, 2), (2, 3), (3, 3))
PACKED = len(BLOCKS) * T
XS = 4
CHUNK = PACKED // XS
PIECE = 64
BF = jnp.bfloat16
F32 = jnp.float32
VMEM_LIMIT = 48 << 20


def params():
    return pltpu.CompilerParams(vmem_limit_bytes=VMEM_LIMIT)


def dot(a, b):
    return lax.dot_general(a, b, (((1,), (0,)), ((), ())), preferred_element_type=F32)


def dot_tn(a, b):
    return lax.dot_general(a, b, (((0,), (0,)), ((), ())), preferred_element_type=F32)


def split(x):
    hi = x.astype(BF)
    return hi, (x - hi.astype(F32)).astype(BF)


def mul(a, b):
    return dot(a[0], b[0]) + (dot(a[0], b[1]) + dot(a[1], b[0]))


def gram_kernel(idx_ref, a_ref, out_ref, acc_ref):
    step = pl.program_id(0)
    upper, lower = a_ref[:, :B], a_ref[:, B:]
    pp, pq, qq = dot_tn(upper, upper), dot_tn(upper, lower), dot_tn(lower, lower)

    @pl.when(step == 0)
    def _():
        acc_ref[0] = pp
        acc_ref[1] = pq
        acc_ref[2] = qq

    @pl.when(step > 0)
    def _():
        acc_ref[0] += pp
        acc_ref[1] += pq
        acc_ref[2] += qq

    @pl.when(step == pl.num_programs(0) - 1)
    def _():
        xi = idx_ref[1]
        for q in range(PACKED // PIECE):
            row, col = BLOCKS[q * PIECE // T]
            part = q * PIECE % T
            which = row // 2 + col // 2
            r0, c0 = row % 2 * T + part, col % 2 * T
            chunk, offset = divmod(q * PIECE, CHUNK)
            place = lax.rem(chunk - xi + XS, XS) * CHUNK + offset
            out_ref[pl.ds(pl.multiple_of(place, PIECE), PIECE), :] = acc_ref[
                which, r0 : r0 + PIECE, c0 : c0 + T
            ]


def gram(slab, pair, xi):
    rows = slab.shape[0]
    tile = 256
    return pl.pallas_call(
        gram_kernel,
        out_shape=jax.ShapeDtypeStruct((PACKED, T), F32),
        grid_spec=pltpu.PrefetchScalarGridSpec(
            num_scalar_prefetch=1,
            grid=(rows // tile,),
            in_specs=[pl.BlockSpec((tile, PAIR), lambda i, idx: (i, idx[0]))],
            out_specs=pl.BlockSpec((PACKED, T), lambda i, idx: (0, 0)),
            scratch_shapes=[pltpu.VMEM((3, B, B), F32)],
        ),
        compiler_params=params(),
        name="gram",
    )(jnp.stack([pair, xi]).astype(jnp.int32), slab)


def inverse(gramian, eye):
    top = jnp.sqrt(jnp.sum(gramian * gramian))
    scale = 2.0 / (2.0 + top)
    gap = scale
    rest = eye - scale * (eye + gramian)

    def more(state):
        count, gap, _, _ = state
        return (gap < 1.0 - 1e-6) & (count < 60)

    def step(state):
        count, gap, rest, approx = state
        rate = 1.0 - gap
        c = 2.0 / (2.0 - rate * rate)
        parts = split(rest)
        square = mul(parts, parts)
        approx = c * (approx + mul(split(approx), parts))
        rest = c * square + (1.0 - c) * eye
        gap = 2.0 * gap * (2.0 - gap) / (1.0 + gap * (2.0 - gap))
        return count + 1, gap, rest, approx

    state = (jnp.int32(0), gap, rest, scale * eye)
    return lax.while_loop(more, step, state)[3]


def rotation_kernel(idx_ref, g0_ref, g1_ref, g2_ref, g3_ref, out_ref, pack_ref, h_ref, e_ref):
    xi = idx_ref[0]
    for i, ref in enumerate((g0_ref, g1_ref, g2_ref, g3_ref)):
        place = lax.rem(xi - i + XS, XS) * CHUNK
        pack_ref[pl.ds(pl.multiple_of(place, PIECE), CHUNK), :] = ref[...]
    for b, (row, col) in enumerate(BLOCKS):
        block = pack_ref[b * T : (b + 1) * T, :]
        h_ref[row * T : (row + 1) * T, col * T : (col + 1) * T] = block
        if row != col:
            h_ref[col * T : (col + 1) * T, row * T : (row + 1) * T] = block.T
    rows = lax.broadcasted_iota(jnp.int32, (B, B), 0)
    cols = lax.broadcasted_iota(jnp.int32, (B, B), 1)
    eye = jnp.where(rows == cols, 1.0, 0.0).astype(F32)

    for sweep in range(INNER):
        trace = jnp.sum((h_ref[:B, :B] + h_ref[B:, B:]) * eye)
        mean = trace / PAIR + 1e-6
        factor = -1.0 / (mean * mean)
        pp, pq = split(h_ref[:B, :B]), split(h_ref[:B, B:])
        qp, qq = split(h_ref[B:, :B]), split(h_ref[B:, B:])
        x = split((mul(pp, pq) - mul(pq, qq)) * factor)
        xt = split((mul(qp, pp) - mul(qq, qp)) * factor)
        pi = inverse(mul(x, xt), eye)
        pis = split(pi)
        w = mul(pis, x)
        wt = mul(xt, pis)
        t = mul(split(wt), x)
        e = jnp.concatenate(
            [
                jnp.concatenate([2.0 * (pi - eye), 2.0 * w], axis=1),
                jnp.concatenate([-2.0 * wt, -2.0 * t], axis=1),
            ],
            axis=0,
        )
        if sweep == 0:
            e_ref[...] = e
            et = jnp.concatenate(
                [
                    jnp.concatenate([2.0 * (pi - eye), -2.0 * w], axis=1),
                    jnp.concatenate([2.0 * wt, -2.0 * t], axis=1),
                ],
                axis=0,
            )
            h = h_ref[...]
            m = h + mul(split(h), split(e))
            h_ref[...] = m + mul(split(et), split(m))
        else:
            first = e_ref[...]
            r = lax.broadcasted_iota(jnp.int32, (PAIR, PAIR), 0)
            c = lax.broadcasted_iota(jnp.int32, (PAIR, PAIR), 1)
            whole = jnp.where(r == c, 1.0, 0.0).astype(F32)
            v = whole + (first + e) + mul(split(first), split(e))
            out_ref[...] = v.astype(BF)


def rotation(chunks, xi):
    spec = pl.BlockSpec((CHUNK, T), lambda i, idx: (0, 0))
    return pl.pallas_call(
        rotation_kernel,
        out_shape=jax.ShapeDtypeStruct((PAIR, PAIR), BF),
        grid_spec=pltpu.PrefetchScalarGridSpec(
            num_scalar_prefetch=1,
            grid=(1,),
            in_specs=[spec] * XS,
            out_specs=pl.BlockSpec((PAIR, PAIR), lambda i, idx: (0, 0)),
            scratch_shapes=[
                pltpu.VMEM((PACKED, T), F32),
                pltpu.VMEM((PAIR, PAIR), F32),
                pltpu.VMEM((PAIR, PAIR), F32),
            ],
        ),
        compiler_params=params(),
        name="rotation",
    )(xi.reshape(1).astype(jnp.int32), *chunks)


def apply_kernel(idx_ref, a_ref, own_ref, other_ref, out_ref, up_ref, down_ref, rot_ref):
    core, position = idx_ref[0], idx_ref[1]

    @pl.when(pl.program_id(0) == 0)
    def _():
        rot_ref[core] = own_ref[...]
        rot_ref[1 - core] = other_ref[...]

    first = dot(a_ref[:, :PAIR], rot_ref[0]).astype(BF)
    second = dot(a_ref[:, PAIR:], rot_ref[1]).astype(BF)
    out_ref[:, :B] = first[:, :B]
    out_ref[:, B:PAIR] = second[:, B:]
    out_ref[:, PAIR + B :] = second[:, :B]

    @pl.when(position == 0)
    def _():
        out_ref[:, PAIR : PAIR + B] = first[:, B:]

    @pl.when(position > 0)
    def _():
        out_ref[:, PAIR : PAIR + B] = first[:, :B]

    up_ref[...] = second[:, :B]
    down_ref[...] = first[:, B:]


def apply(slab, own, other, core, position):
    rows, cols = slab.shape
    tile = 256
    fixed = pl.BlockSpec((PAIR, PAIR), lambda i, idx: (0, 0))
    half = pl.BlockSpec((tile, B), lambda i, idx: (i, 0))
    full = pl.BlockSpec((tile, cols), lambda i, idx: (i, 0))
    return pl.pallas_call(
        apply_kernel,
        out_shape=(
            jax.ShapeDtypeStruct((rows, cols), BF),
            jax.ShapeDtypeStruct((rows, B), BF),
            jax.ShapeDtypeStruct((rows, B), BF),
        ),
        grid_spec=pltpu.PrefetchScalarGridSpec(
            num_scalar_prefetch=1,
            grid=(rows // tile,),
            in_specs=[full, fixed, fixed],
            out_specs=(full, half, half),
            scratch_shapes=[pltpu.VMEM((2, PAIR, PAIR), BF)],
        ),
        compiler_params=params(),
        name="apply",
    )(jnp.stack([core, position]).astype(jnp.int32), slab, own, other)


def finish_kernel(last, idx_ref, before_ref, after_ref, part_ref, out_ref, sems):
    del part_ref
    position = idx_ref[0]

    def low():
        return pltpu.make_async_copy(before_ref, out_ref.at[:, pl.ds(0, B)], sems.at[0])

    def high():
        return pltpu.make_async_copy(after_ref, out_ref.at[:, pl.ds(PAIR + B, B)], sems.at[1])

    @pl.when(position > 0)
    def _():
        low().start()

    @pl.when(position < last)
    def _():
        high().start()

    @pl.when(position > 0)
    def _():
        low().wait()

    @pl.when(position < last)
    def _():
        high().wait()


def finish(part, before, after, position, last):
    anywhere = pl.BlockSpec(memory_space=pl.ANY)
    return pl.pallas_call(
        lambda *refs: finish_kernel(last, *refs),
        out_shape=jax.ShapeDtypeStruct(part.shape, part.dtype),
        grid_spec=pltpu.PrefetchScalarGridSpec(
            num_scalar_prefetch=1,
            grid=(1,),
            in_specs=[anywhere] * 3,
            out_specs=anywhere,
            scratch_shapes=[pltpu.SemaphoreType.DMA((2,))],
        ),
        input_output_aliases={3: 0},
        compiler_params=params(),
        name="finish",
    )(position.reshape(1).astype(jnp.int32), before, after, part)


def shifted(array, axis, by):
    size = lax.axis_size(axis)
    return lax.ppermute(array, axis, [(i, (i + by) % size) for i in range(size)])


def body(slab):
    core, xi = lax.axis_index("core"), lax.axis_index("x")
    chain = ("blk", "grp")
    size, position = lax.axis_size(chain), lax.axis_index(chain)

    theirs = gram(slab, 1 - core, xi)
    received = shifted(theirs, "core", 1)
    packed = gram(slab, core, xi) + received

    total = packed[:CHUNK]
    parts = [
        shifted(packed[i * CHUNK : (i + 1) * CHUNK], "x", i) for i in range(1, XS)
    ]
    total = total + parts[0] + parts[1] + parts[2]
    total = total + shifted(total, "yh", 1)
    chunks = [total] + [shifted(total, "x", i) for i in range(1, XS)]

    own = rotation(chunks, xi)
    other = shifted(own, "core", 1)
    part, up, down = apply(slab, own, other, core, position)
    before = lax.ppermute(up, chain, [(i, i + 1) for i in range(size - 1)])
    after = lax.ppermute(down, chain, [(i, i - 1) for i in range(1, size)])
    return finish(part, before, after, position, size - 1)


def solution(mesh):
    rows, blk, grp = (mesh.shape[name] for name in ("row", "blk", "grp"))
    fine = Mesh(
        mesh.devices.reshape(rows // (2 * XS), XS, 2, blk, grp),
        ("yh", "x", "core", "blk", "grp"),
    )
    spec = P(("yh", "x", "core"), ("blk", "grp"))
    return jax.shard_map(
        body, mesh=fine, in_specs=(spec,), out_specs=spec, check_vma=False
    )
```

time: 879 us -> 74.4 us (0.08); the launches traced: 869 us -> 74 us
  other arithmetic: 455 us -> 0.35 us
  local copies, waits for them, and re-layouts: 171 us -> 1.63 us
  waiting for transfers between devices: 157 us -> 33.1 us
  matrix products: 63.2 us -> 0 us
  Pallas kernels: 0 us -> 20.2 us
  between operations: 14.4 us -> 0.1 us
  starting transfers between devices: 7.29 us -> 18.6 us
    another operation x38 -> x3, other arithmetic: 447 us -> 0.23 us  [the longest x2 0.15 us: gram(): jnp.stack([pair, xi]).astype(jnp.int32)]
    psum x1 -> x0, waiting for transfers between devices: 144 us -> none  [body(): gram_blocks = lax.psum(gram_local, 'row')]
    dot_general x3 -> x0, local copies, waits for them, and re-layouts: 61.5 us -> none  [batched_dot(): jnp.einsum('pij,pjk->pik', left_side, right_side, precision=lax.Precision...]
    psum x1 -> x0, local copies, waits for them, and re-layouts: 60.2 us -> none  [body(): gram_blocks = lax.psum(gram_local, 'row')]
    another operation x32 -> x0, matrix products: 32.9 us -> none  [the longest x12 11.3 us: cayley(): jax.scipy.linalg.cho_solve((factor_right, True), jnp.concatenate([2.0 * f...]
    dot_general x13 -> x0, matrix products: 30.3 us -> none  [the longest x11 24 us: batched_dot(): jnp.einsum('pij,pjk->pik', left_side, right_side, precision=lax.Precision...]
    another operation x37 -> x0, local copies, waits for them, and re-layouts: 26.9 us -> none  [the longest x17 12.9 us: cayley(): jax.scipy.linalg.cho_solve((factor_left, True), jnp.concatenate([identity...]
    pallas_call x0 -> x5, Pallas kernels: none -> 20.2 us  [the longest x1 11.1 us: rotation(): pl.pallas_call(rotation_kernel, out_shape=jax.ShapeDtypeStruct((PAIR, PAI...]
  transfers between devices with their start and end apart: 3 -> 11, of which waited for: 3 -> 10; matrix products, arithmetic and copies ran while one was open for 0% -> 0% of each run, Pallas kernels for 0% -> 3%
where the time goes in v1:
time: 74.4 us; the launch traced here: 74 us
  waiting for transfers between devices  33.1 us (44%)
  Pallas kernels  20.2 us (27%)
  starting transfers between devices  18.6 us (25%)
  local copies, waits for them, and re-layouts  1.63 us (2%)
    ppermute x9, waiting for transfers between devices, shifted(): lax.ppermute(array, axis, [(i, (i + by) % size) for i in range(size)])  21.4 us
    pallas_call x1, Pallas kernels, rotation(): pl.pallas_call(rotation_kernel, out_shape=jax.ShapeDtypeStruct((PAIR, PAI...  11.1 us
    ppermute x9, starting transfers between devices, shifted(): lax.ppermute(array, axis, [(i, (i + by) % size) for i in range(size)])  10.7 us
    ppermute x1, waiting for transfers between devices, body(): before = lax.ppermute(up, chain, [(i, i + 1) for i in range(size - 1)])  10.1 us
    pallas_call x2, Pallas kernels, gram(): pl.pallas_call(gram_kernel, out_shape=jax.ShapeDtypeStruct((PACKED, T), F...  4.48 us
    ppermute x1, starting transfers between devices, body(): after = lax.ppermute(down, chain, [(i, i - 1) for i in range(1, size)])  4.13 us
    ppermute x1, starting transfers between devices, body(): before = lax.ppermute(up, chain, [(i, i + 1) for i in range(size - 1)])  3.81 us
    pallas_call x1, Pallas kernels, apply(): pl.pallas_call(apply_kernel, out_shape=(jax.ShapeDtypeStruct((rows, cols)...  3.66 us
  transfers between devices with their start and end apart: 11, of which 10 were waited for; matrix products, arithmetic and copies ran while one was open for 0% of the time, Pallas kernels for 3%

profile of v1, /device:TPU:8, one launch (start us, length us, event | category | flops | bytes accessed | tf_op | source)
XLA Modules:
  0.0 74.0 jit_solution(6705166382411394025)
XLA Ops:
  0.1 1.6 %copy-done = bf16[1024,1024]{1,0:T(8,128)(2,1)S(1)} copy-done((bf16[1024,1024]{1,0:T(8,128)(2,1)S(1)}, bf16[1024,1024]{1,0:T(8,128)(2,1)}, u32[]{:S(2)}) %copy-start) | copy-done | bytes 2097176
  1.7 2.2 %gram.3 = f32[1280,128]{1,0:T(8,128)S(1)} custom-call(s32[2]{0:T(128)S(1)} %pad_add_fusion.1.idx_ref, bf16[1024,1024]{1,0:T(8,128)(2,1)S(1)} %copy-done), custom_call_target="tpu_custom_call" | custom-call | tf_op jit(solution)/shard_map/gram/pallas_call | solution.py:78
  4.1 2.2 %gram.2 = f32[1280,128]{1,0:T(8,128)S(1)} custom-call(s32[2]{0:T(128)S(1)} %pad_add_fusion.2.idx_ref, bf16[1024,1024]{1,0:T(8,128)(2,1)S(1)} %copy-done.1), custom_call_target="tpu_custom_call" | custom-call | tf_op jit(solution)/shard_map/gram/pallas_call | solution.py:78
  6.5 1.6 %collective-permute-start.1 = (f32[320,128]{1,0:T(8,128)S(1)}, f32[320,128]{1,0:T(8,128)S(1)}, u32[]{:S(2)}, u32[]{:S(2)}) collective-permute-start(f32[320,128]{1,0:T(8,128)S(1)} %get-tuple-element.11), channel_id=1, source_target_pairs={{0,16},{16,32},{32,48},{48,0},{1,17},{17,33},{33,49},{49,1},{2,18}... | collective-permute-start | bytes 491528 | tf_op jit(solution)/shard_map/ppermute | solution.py:292
  8.0 1.7 %collective-permute-start.3 = (f32[320,128]{1,0:T(8,128)S(1)}, f32[320,128]{1,0:T(8,128)S(1)}, u32[]{:S(2)}, u32[]{:S(2)}) collective-permute-start(f32[320,128]{1,0:T(8,128)S(1)} %get-tuple-element.12), channel_id=1, source_target_pairs={{0,48},{16,0},{32,16},{48,32},{1,49},{17,1},{33,17},{49,33},{2,50}... | collective-permute-start | bytes 491528 | tf_op jit(solution)/shard_map/ppermute | solution.py:292
  9.8 1.8 %collective-permute-start.2 = (f32[320,128]{1,0:T(8,128)S(1)}, f32[320,128]{1,0:T(8,128)S(1)}, u32[]{:S(2)}, u32[]{:S(2)}) collective-permute-start(f32[320,128]{1,0:T(8,128)S(1)} %get-tuple-element.13), channel_id=1, source_target_pairs={{0,32},{16,48},{32,0},{48,16},{1,33},{17,49},{33,1},{49,17},{2,34}... | collective-permute-start | bytes 491528 | tf_op jit(solution)/shard_map/ppermute | solution.py:292
  11.6 2.8 %collective-permute-done.1 = f32[320,128]{1,0:T(8,128)S(1)} collective-permute-done((f32[320,128]{1,0:T(8,128)S(1)}, f32[320,128]{1,0:T(8,128)S(1)}, u32[]{:S(2)}, u32[]{:S(2)}) %collective-permute-start.1) | collective-permute-done | bytes 163872 | tf_op jit(solution)/shard_map/ppermute | solution.py:292
  14.4 2.8 %collective-permute-done.3 = f32[320,128]{1,0:T(8,128)S(1)} collective-permute-done((f32[320,128]{1,0:T(8,128)S(1)}, f32[320,128]{1,0:T(8,128)S(1)}, u32[]{:S(2)}, u32[]{:S(2)}) %collective-permute-start.3) | collective-permute-done | bytes 163872 | tf_op jit(solution)/shard_map/ppermute | solution.py:292
  17.2 1.7 %collective-permute-done.2 = f32[320,128]{1,0:T(8,128)S(1)} collective-permute-done((f32[320,128]{1,0:T(8,128)S(1)}, f32[320,128]{1,0:T(8,128)S(1)}, u32[]{:S(2)}, u32[]{:S(2)}) %collective-permute-start.2) | collective-permute-done | bytes 163872 | tf_op jit(solution)/shard_map/ppermute | solution.py:292
  18.9 2.4 %collective-permute-start.4 = (f32[320,128]{1,0:T(8,128)S(1)}, f32[320,128]{1,0:T(8,128)S(1)}, u32[]{:S(2)}, u32[]{:S(2)}) collective-permute-start(f32[320,128]{1,0:T(8,128)S(1)} %fusion.1), channel_id=1, source_target_pairs={{0,64},{64,0},{1,65},{65,1},{2,66},{66,2},{3,67},{67,3},{4,68},{68... | collective-permute-start | bytes 491528 | tf_op jit(solution)/shard_map/ppermute | solution.py:292
  21.3 5.0 %collective-permute-done.4 = f32[320,128]{1,0:T(8,128)S(1)} collective-permute-done((f32[320,128]{1,0:T(8,128)S(1)}, f32[320,128]{1,0:T(8,128)S(1)}, u32[]{:S(2)}, u32[]{:S(2)}) %collective-permute-start.4) | collective-permute-done | bytes 163872 | tf_op jit(solution)/shard_map/ppermute | solution.py:292
  26.2 1.6 %collective-permute-start.7 = (f32[320,128]{1,0:T(8,128)S(1)}, f32[320,128]{1,0:T(8,128)S(1)}, u32[]{:S(2)}, u32[]{:S(2)}) collective-permute-start(f32[320,128]{1,0:T(8,128)S(1)} %add.23.g0_ref), channel_id=1, source_target_pairs={{0,48},{16,0},{32,16},{48,32},{1,49},{17,1},{33,17},{49,33},{2,50}... | collective-permute-start | bytes 491528 | tf_op jit(solution)/shard_map/ppermute | solution.py:292
  27.9 1.4 %collective-permute-start.6 = (f32[320,128]{1,0:T(8,128)S(1)}, f32[320,128]{1,0:T(8,128)S(1)}, u32[]{:S(2)}, u32[]{:S(2)}) collective-permute-start(f32[320,128]{1,0:T(8,128)S(1)} %add.23.g0_ref), channel_id=1, source_target_pairs={{0,32},{16,48},{32,0},{48,16},{1,33},{17,49},{33,1},{49,17},{2,34}... | collective-permute-start | bytes 491528 | tf_op jit(solution)/shard_map/ppermute | solution.py:292
  29.2 3.7 %collective-permute-done.7.g3_ref = f32[320,128]{1,0:T(8,128)S(1)} collective-permute-done((f32[320,128]{1,0:T(8,128)S(1)}, f32[320,128]{1,0:T(8,128)S(1)}, u32[]{:S(2)}, u32[]{:S(2)}) %collective-permute-start.7) | collective-permute-done | bytes 163872 | tf_op jit(solution)/shard_map/ppermute | solution.py:292
  32.9 2.1 %collective-permute-done.6.g2_ref = f32[320,128]{1,0:T(8,128)S(1)} collective-permute-done((f32[320,128]{1,0:T(8,128)S(1)}, f32[320,128]{1,0:T(8,128)S(1)}, u32[]{:S(2)}, u32[]{:S(2)}) %collective-permute-start.6) | collective-permute-done | bytes 163872 | tf_op jit(solution)/shard_map/ppermute | solution.py:292
  35.0 1.7 %collective-permute-done.5.g1_ref = f32[320,128]{1,0:T(8,128)S(1)} collective-permute-done((f32[320,128]{1,0:T(8,128)S(1)}, f32[320,128]{1,0:T(8,128)S(1)}, u32[]{:S(2)}, u32[]{:S(2)}) %collective-permute-start.5) | collective-permute-done | bytes 163872 | tf_op jit(solution)/shard_map/ppermute | solution.py:292
  36.7 11.1 %rotation.1.own_ref = bf16[512,512]{1,0:T(8,128)(2,1)S(1)} custom-call(s32[1]{0:T(128)} %bitcast.2.idx_ref, f32[320,128]{1,0:T(8,128)S(1)} %add.23.g0_ref, f32[320,128]{1,0:T(8,128)S(1)} %collective-permute-done.5.g1_ref, f32[320,128]{1,0:T(8,128)S(1)} %collective-permute-done.6.g2_ref, f32[320,128]{1,0:T(8,128)S(1)} %collective-permute-done.7.g3_ref), custom_call_target="tpu_custom_call" | custom-call | tf_op jit(solution)/shard_map/rotation/pallas_call | solution.py:175
  47.9 1.8 %collective-permute-done.8.other_ref = bf16[512,512]{1,0:T(8,128)(2,1)S(1)} collective-permute-done((bf16[512,512]{1,0:T(8,128)(2,1)S(1)}, bf16[512,512]{1,0:T(8,128)(2,1)S(1)}, u32[]{:S(2)}, u32[]{:S(2)}) %collective-permute-start.8) | collective-permute-done | bytes 524320 | tf_op jit(solution)/shard_map/ppermute | solution.py:292
  49.8 3.7 %apply.1 = (bf16[1024,1024]{1,0:T(8,128)(2,1)}, bf16[1024,256]{1,0:T(8,128)(2,1)S(1)}, bf16[1024,256]{1,0:T(8,128)(2,1)S(1)}) custom-call(s32[2]{0:T(128)S(1)} %pad_add_fusion.idx_ref, bf16[1024,1024]{1,0:T(8,128)(2,1)S(1)} %copy-done.1, bf16[512,512]{1,0:T(8,128)(2,1)S(1)} %rotation.1.own_ref, bf16[512,512]{1,0:T(8,128)(2,1)S(1)} %collective-permute-done.8.other_ref), custom_call_target="tpu_custom_call" | custom-call | tf_op jit(solution)/shard_map/apply/pallas_call | solution.py:226
  53.4 3.8 %collective-permute-start.9 = (bf16[1024,256]{1,0:T(8,128)(2,1)S(1)}, bf16[1024,256]{1,0:T(8,128)(2,1)S(1)}, u32[]{:S(2)}, u32[]{:S(2)}) collective-permute-start(bf16[1024,256]{1,0:T(8,128)(2,1)S(1)} %get-tuple-element.8), channel_id=1, source_target_pairs={{0,1},{1,2},{2,3},{3,4},{4,5},{5,6},{6,7},{8,9},{9,10},{10,11},{11... | collective-permute-start | bytes 1572872 | tf_op jit(solution)/shard_map/ppermute | solution.py:315
  57.2 4.1 %collective-permute-start.10 = (bf16[1024,256]{1,0:T(8,128)(2,1)S(1)}, bf16[1024,256]{1,0:T(8,128)(2,1)S(1)}, u32[]{:S(2)}, u32[]{:S(2)}) collective-permute-start(bf16[1024,256]{1,0:T(8,128)(2,1)S(1)} %get-tuple-element.9), channel_id=1, source_target_pairs={{1,0},{2,1},{3,2},{4,3},{5,4},{6,5},{7,6},{9,8},{10,9},{11,10},{12... | collective-permute-start | bytes 1572872 | tf_op jit(solution)/shard_map/ppermute | solution.py:316
  61.4 10.1 %collective-permute-done.9.refs_1_ = bf16[1024,256]{1,0:T(8,128)(2,1)S(1)} collective-permute-done((bf16[1024,256]{1,0:T(8,128)(2,1)S(1)}, bf16[1024,256]{1,0:T(8,128)(2,1)S(1)}, u32[]{:S(2)}, u32[]{:S(2)}) %collective-permute-start.9) | collective-permute-done | bytes 524320 | tf_op jit(solution)/shard_map/ppermute | solution.py:315
  71.4 1.6 %collective-permute-done.10.refs_2_ = bf16[1024,256]{1,0:T(8,128)(2,1)S(1)} collective-permute-done((bf16[1024,256]{1,0:T(8,128)(2,1)S(1)}, bf16[1024,256]{1,0:T(8,128)(2,1)S(1)}, u32[]{:S(2)}, u32[]{:S(2)}) %collective-permute-start.10) | collective-permute-done | bytes 524320 | tf_op jit(solution)/shard_map/ppermute | solution.py:316
  73.0 1.0 %finish.1 = bf16[1024,1024]{1,0:T(8,128)(2,1)} custom-call(s32[1]{0:T(128)} %bitcast.refs_0_, bf16[1024,256]{1,0:T(8,128)(2,1)S(1)} %collective-permute-done.9.refs_1_, bf16[1024,256]{1,0:T(8,128)(2,1)S(1)} %collective-permute-done.10.refs_2_, bf16[1024,1024]{1,0:T(8,128)(2,1)} %get-tuple-element.10.refs_3_), custom_call_target="tpu_custom_call", output_to_operand_aliasing={{}: (3, {})} | custom-call | tf_op jit(solution)/shard_map/finish/pallas_call | solution.py:274
  (14 shorter events, 0.6 us)
Async XLA Ops:
  0.1 1.6 %copy-start = (bf16[1024,1024]{1,0:T(8,128)(2,1)S(1)}, bf16[1024,1024]{1,0:T(8,128)(2,1)}, u32[]{:S(2)}) copy-start(bf16[1024,1024]{1,0:T(8,128)(2,1)} %a_ref.5) | copy-start | bytes 6291460
  1.7 2.4 %copy-start.1 = (bf16[1024,1024]{1,0:T(8,128)(2,1)S(1)}, bf16[1024,1024]{1,0:T(8,128)(2,1)}, u32[]{:S(2)}) copy-start(bf16[1024,1024]{1,0:T(8,128)(2,1)} %a_ref.5) | copy-start | bytes 6291460
  3.9 2.4 %collective-permute-start = (f32[1280,128]{1,0:T(8,128)S(1)}, f32[1280,128]{1,0:T(8,128)S(1)}, u32[]{:S(2)}, u32[]{:S(2)}) collective-permute-start(f32[1280,128]{1,0:T(8,128)S(1)} %gram.3), channel_id=1, source_target_pairs={{0,8},{8,0},{1,9},{9,1},{2,10},{10,2},{3,11},{11,3},{4,12},{12,4},... | collective-permute-start | bytes 1966088 | tf_op jit(solution)/shard_map/ppermute | solution.py:292
  6.5 7.9 %collective-permute-start.1 = (f32[320,128]{1,0:T(8,128)S(1)}, f32[320,128]{1,0:T(8,128)S(1)}, u32[]{:S(2)}, u32[]{:S(2)}) collective-permute-start(f32[320,128]{1,0:T(8,128)S(1)} %get-tuple-element.11), channel_id=1, source_target_pairs={{0,16},{16,32},{32,48},{48,0},{1,17},{17,33},{33,49},{49,1},{2,18}... | collective-permute-start | bytes 491528 | tf_op jit(solution)/shard_map/ppermute | solution.py:292
  8.0 9.1 %collective-permute-start.3 = (f32[320,128]{1,0:T(8,128)S(1)}, f32[320,128]{1,0:T(8,128)S(1)}, u32[]{:S(2)}, u32[]{:S(2)}) collective-permute-start(f32[320,128]{1,0:T(8,128)S(1)} %get-tuple-element.12), channel_id=1, source_target_pairs={{0,48},{16,0},{32,16},{48,32},{1,49},{17,1},{33,17},{49,33},{2,50}... | collective-permute-start | bytes 491528 | tf_op jit(solution)/shard_map/ppermute | solution.py:292
  9.8 9.1 %collective-permute-start.2 = (f32[320,128]{1,0:T(8,128)S(1)}, f32[320,128]{1,0:T(8,128)S(1)}, u32[]{:S(2)}, u32[]{:S(2)}) collective-permute-start(f32[320,128]{1,0:T(8,128)S(1)} %get-tuple-element.13), channel_id=1, source_target_pairs={{0,32},{16,48},{32,0},{48,16},{1,33},{17,49},{33,1},{49,17},{2,34}... | collective-permute-start | bytes 491528 | tf_op jit(solution)/shard_map/ppermute | solution.py:292
  18.9 7.3 %collective-permute-start.4 = (f32[320,128]{1,0:T(8,128)S(1)}, f32[320,128]{1,0:T(8,128)S(1)}, u32[]{:S(2)}, u32[]{:S(2)}) collective-permute-start(f32[320,128]{1,0:T(8,128)S(1)} %fusion.1), channel_id=1, source_target_pairs={{0,64},{64,0},{1,65},{65,1},{2,66},{66,2},{3,67},{67,3},{4,68},{68... | collective-permute-start | bytes 491528 | tf_op jit(solution)/shard_map/ppermute | solution.py:292
  26.2 6.7 %collective-permute-start.7 = (f32[320,128]{1,0:T(8,128)S(1)}, f32[320,128]{1,0:T(8,128)S(1)}, u32[]{:S(2)}, u32[]{:S(2)}) collective-permute-start(f32[320,128]{1,0:T(8,128)S(1)} %add.23.g0_ref), channel_id=1, source_target_pairs={{0,48},{16,0},{32,16},{48,32},{1,49},{17,1},{33,17},{49,33},{2,50}... | collective-permute-start | bytes 491528 | tf_op jit(solution)/shard_map/ppermute | solution.py:292
  27.9 7.2 %collective-permute-start.6 = (f32[320,128]{1,0:T(8,128)S(1)}, f32[320,128]{1,0:T(8,128)S(1)}, u32[]{:S(2)}, u32[]{:S(2)}) collective-permute-start(f32[320,128]{1,0:T(8,128)S(1)} %add.23.g0_ref), channel_id=1, source_target_pairs={{0,32},{16,48},{32,0},{48,16},{1,33},{17,49},{33,1},{49,17},{2,34}... | collective-permute-start | bytes 491528 | tf_op jit(solution)/shard_map/ppermute | solution.py:292
  29.2 7.4 %collective-permute-start.5 = (f32[320,128]{1,0:T(8,128)S(1)}, f32[320,128]{1,0:T(8,128)S(1)}, u32[]{:S(2)}, u32[]{:S(2)}) collective-permute-start(f32[320,128]{1,0:T(8,128)S(1)} %add.23.g0_ref), channel_id=1, source_target_pairs={{0,16},{16,32},{32,48},{48,0},{1,17},{17,33},{33,49},{49,1},{2,18}... | collective-permute-start | bytes 491528 | tf_op jit(solution)/shard_map/ppermute | solution.py:292
  47.8 2.0 %collective-permute-start.8 = (bf16[512,512]{1,0:T(8,128)(2,1)S(1)}, bf16[512,512]{1,0:T(8,128)(2,1)S(1)}, u32[]{:S(2)}, u32[]{:S(2)}) collective-permute-start(bf16[512,512]{1,0:T(8,128)(2,1)S(1)} %rotation.1.own_ref), channel_id=1, source_target_pairs={{0,8},{8,0},{1,9},{9,1},{2,10},{10,2},{3,11},{11,3},{4,12},{12,4},... | collective-permute-start | bytes 1572872 | tf_op jit(solution)/shard_map/ppermute | solution.py:292
  53.4 18.0 %collective-permute-start.9 = (bf16[1024,256]{1,0:T(8,128)(2,1)S(1)}, bf16[1024,256]{1,0:T(8,128)(2,1)S(1)}, u32[]{:S(2)}, u32[]{:S(2)}) collective-permute-start(bf16[1024,256]{1,0:T(8,128)(2,1)S(1)} %get-tuple-element.8), channel_id=1, source_target_pairs={{0,1},{1,2},{2,3},{3,4},{4,5},{5,6},{6,7},{8,9},{9,10},{10,11},{11... | collective-permute-start | bytes 1572872 | tf_op jit(solution)/shard_map/ppermute | solution.py:315
  57.2 15.8 %collective-permute-start.10 = (bf16[1024,256]{1,0:T(8,128)(2,1)S(1)}, bf16[1024,256]{1,0:T(8,128)(2,1)S(1)}, u32[]{:S(2)}, u32[]{:S(2)}) collective-permute-start(bf16[1024,256]{1,0:T(8,128)(2,1)S(1)} %get-tuple-element.9), channel_id=1, source_target_pairs={{1,0},{2,1},{3,2},{4,3},{5,4},{6,5},{7,6},{9,8},{10,9},{11,10},{12... | collective-permute-start | bytes 1572872 | tf_op jit(solution)/shard_map/ppermute | solution.py:316

commit v2 on v1

--- a/solution.py
+++ b/solution.py
@@ -4,6 +4,7 @@
 from jax.experimental import pallas as pl
 from jax.experimental.pallas import tpu as pltpu
 from jax.sharding import Mesh, PartitionSpec as P
+
 
 B = 256
 PAIR = 2 * B
@@ -14,9 +15,13 @@
 XS = 4
 CHUNK = PACKED // XS
 PIECE = 64
+TAIL = 16
+SPAN = CHUNK + TAIL
 BF = jnp.bfloat16
 F32 = jnp.float32
 VMEM_LIMIT = 48 << 20
+ROW_TILE = 256
+TOP_EXPONENT = 14.0
 
 
 def params():
@@ -60,16 +65,21 @@
     @pl.when(step == pl.num_programs(0) - 1)
     def _():
         xi = idx_ref[1]
+        top = jnp.zeros((TAIL, T), F32)
         for q in range(PACKED // PIECE):
             row, col = BLOCKS[q * PIECE // T]
             part = q * PIECE % T
             which = row // 2 + col // 2
             r0, c0 = row % 2 * T + part, col % 2 * T
             chunk, offset = divmod(q * PIECE, CHUNK)
-            place = lax.rem(chunk - xi + XS, XS) * CHUNK + offset
-            out_ref[pl.ds(pl.multiple_of(place, PIECE), PIECE), :] = acc_ref[
-                which, r0 : r0 + PIECE, c0 : c0 + T
-            ]
+            place = lax.rem(chunk - xi + XS, XS) * SPAN + offset
+            piece = acc_ref[which, r0 : r0 + PIECE, c0 : c0 + T]
+            out_ref[pl.ds(pl.multiple_of(place, TAIL), PIECE), :] = piece
+            for r in range(0, PIECE, TAIL):
+                top = jnp.maximum(top, jnp.abs(piece[r : r + TAIL]))
+        top = jnp.broadcast_to(jnp.max(top, axis=0, keepdims=True), (TAIL, T))
+        for i in range(XS):
+            out_ref[i * SPAN + CHUNK : (i + 1) * SPAN, :] = top
 
 
 def gram(slab, pair, xi):
@@ -77,12 +87,12 @@
     tile = 256
     return pl.pallas_call(
         gram_kernel,
-        out_shape=jax.ShapeDtypeStruct((PACKED, T), F32),
+        out_shape=jax.ShapeDtypeStruct((XS * SPAN, T), F32),
         grid_spec=pltpu.PrefetchScalarGridSpec(
             num_scalar_prefetch=1,
             grid=(rows // tile,),
             in_specs=[pl.BlockSpec((tile, PAIR), lambda i, idx: (i, idx[0]))],
-            out_specs=pl.BlockSpec((PACKED, T), lambda i, idx: (0, 0)),
+            out_specs=pl.BlockSpec((XS * SPAN, T), lambda i, idx: (0, 0)),
             scratch_shapes=[pltpu.VMEM((3, B, B), F32)],
         ),
         compiler_params=params(),
@@ -119,7 +129,7 @@
     xi = idx_ref[0]
     for i, ref in enumerate((g0_ref, g1_ref, g2_ref, g3_ref)):
         place = lax.rem(xi - i + XS, XS) * CHUNK
-        pack_ref[pl.ds(pl.multiple_of(place, PIECE), CHUNK), :] = ref[...]
+        pack_ref[pl.ds(pl.multiple_of(place, PIECE), CHUNK), :] = ref[:CHUNK, :]
     for b, (row, col) in enumerate(BLOCKS):
         block = pack_ref[b * T : (b + 1) * T, :]
         h_ref[row * T : (row + 1) * T, col * T : (col + 1) * T] = block
@@ -171,7 +181,7 @@
 
 
 def rotation(chunks, xi):
-    spec = pl.BlockSpec((CHUNK, T), lambda i, idx: (0, 0))
+    spec = pl.BlockSpec((SPAN, T), lambda i, idx: (0, 0))
     return pl.pallas_call(
         rotation_kernel,
         out_shape=jax.ShapeDtypeStruct((PAIR, PAIR), BF),
@@ -191,100 +201,144 @@
     )(xi.reshape(1).astype(jnp.int32), *chunks)
 
 
-def apply_kernel(idx_ref, a_ref, own_ref, other_ref, out_ref, up_ref, down_ref, rot_ref):
+def whole(count):
+    return [pl.BlockSpec(memory_space=pltpu.VMEM)] * count
+
+
+def numbers(*values):
+    return jnp.stack(values).astype(jnp.int32)
+
+
+SCALARS = pl.BlockSpec(memory_space=pltpu.SMEM)
+ANYWHERE = pl.BlockSpec(memory_space=pl.ANY)
+
+
+def row_tiles(rows):
+    return [pl.ds(i * ROW_TILE, ROW_TILE) for i in range(rows // ROW_TILE)]
+
+
+def edge_kernel(idx_ref, a_ref, rot_ref, out_ref):
+    columns = pl.ds(pl.multiple_of(idx_ref[0] * PAIR, PAIR), PAIR)
+    rot = rot_ref[:, pl.ds(pl.multiple_of(idx_ref[1] * B, B), B)]
+    for tile in row_tiles(a_ref.shape[0]):
+        out_ref[tile, :] = dot(a_ref[tile, columns], rot).astype(BF)
+
+
+def edge(slab, rot, pair, half):
+    return pl.pallas_call(
+        edge_kernel,
+        out_shape=jax.ShapeDtypeStruct((slab.shape[0], B), BF),
+        in_specs=[SCALARS] + whole(2),
+        out_specs=whole(1)[0],
+        compiler_params=params(),
+        name="edge",
+    )(numbers(pair, half), slab, rot)
+
+
+def inner_kernel(last, idx_ref, a_ref, own_ref, other_ref, first_ref, out_ref, rot_ref, stage_ref, sems):
     core, position = idx_ref[0], idx_ref[1]
-
-    @pl.when(pl.program_id(0) == 0)
-    def _():
-        rot_ref[core] = own_ref[...]
-        rot_ref[1 - core] = other_ref[...]
-
-    first = dot(a_ref[:, :PAIR], rot_ref[0]).astype(BF)
-    second = dot(a_ref[:, PAIR:], rot_ref[1]).astype(BF)
-    out_ref[:, :B] = first[:, :B]
-    out_ref[:, B:PAIR] = second[:, B:]
-    out_ref[:, PAIR + B :] = second[:, :B]
-
-    @pl.when(position == 0)
-    def _():
-        out_ref[:, PAIR : PAIR + B] = first[:, B:]
-
-    @pl.when(position > 0)
-    def _():
-        out_ref[:, PAIR : PAIR + B] = first[:, :B]
-
-    up_ref[...] = second[:, :B]
-    down_ref[...] = first[:, B:]
-
-
-def apply(slab, own, other, core, position):
-    rows, cols = slab.shape
-    tile = 256
-    fixed = pl.BlockSpec((PAIR, PAIR), lambda i, idx: (0, 0))
-    half = pl.BlockSpec((tile, B), lambda i, idx: (i, 0))
-    full = pl.BlockSpec((tile, cols), lambda i, idx: (i, 0))
+    tiles = row_tiles(a_ref.shape[0])
+
+    def arrived(side):
+        return pltpu.make_async_copy(
+            first_ref, out_ref.at[:, pl.ds(side * (PAIR + B), B)], sems.at[len(tiles)]
+        )
+
+    def ended(i, side):
+        columns = pl.ds(side * (PAIR + B), B)
+        return pltpu.make_async_copy(
+            stage_ref.at[tiles[i], columns],
+            out_ref.at[tiles[i], columns],
+            sems.at[len(tiles) + 1 + i],
+        )
+
+    goes = ((core == 1) & (position > 0), (core == 0) & (position < last))
+    for side in range(2):
+
+        @pl.when(goes[side])
+        def _():
+            arrived(side).start()
+
+    rot_ref[core] = own_ref[...]
+    rot_ref[1 - core] = other_ref[...]
+    kept = rot_ref[1, :, B:]
+    passed = rot_ref[0, :, pl.ds(pl.multiple_of(jnp.where(position == 0, B, 0), B), B)]
+    middle = pl.ds(B, PAIR)
+    copies = []
+    for i, tile in enumerate(tiles):
+        stage_ref[tile, B:PAIR] = dot(a_ref[tile, PAIR:], kept).astype(BF)
+        stage_ref[tile, PAIR : PAIR + B] = dot(a_ref[tile, :PAIR], passed).astype(BF)
+        copies.append(
+            pltpu.make_async_copy(
+                stage_ref.at[tile, middle], out_ref.at[tile, middle], sems.at[i]
+            )
+        )
+        copies[-1].start()
+    for side, place in ((0, 0), (1, last)):
+
+        @pl.when(position == place)
+        def _():
+            rot = rot_ref[side, :, :B]
+            for i, tile in enumerate(tiles):
+                pair = a_ref[tile, side * PAIR : (side + 1) * PAIR]
+                columns = slice(side * (PAIR + B), side * (PAIR + B) + B)
+                stage_ref[tile, columns] = dot(pair, rot).astype(BF)
+                ended(i, side).start()
+            for i in range(len(tiles)):
+                ended(i, side).wait()
+
+    for copy in copies:
+        copy.wait()
+    for side in range(2):
+
+        @pl.when(goes[side])
+        def _():
+            arrived(side).wait()
+
+
+def inner(slab, own, other, first, core, position, last):
+    count = slab.shape[0] // ROW_TILE
     return pl.pallas_call(
-        apply_kernel,
-        out_shape=(
-            jax.ShapeDtypeStruct((rows, cols), BF),
-            jax.ShapeDtypeStruct((rows, B), BF),
-            jax.ShapeDtypeStruct((rows, B), BF),
-        ),
-        grid_spec=pltpu.PrefetchScalarGridSpec(
-            num_scalar_prefetch=1,
-            grid=(rows // tile,),
-            in_specs=[full, fixed, fixed],
-            out_specs=(full, half, half),
-            scratch_shapes=[pltpu.VMEM((2, PAIR, PAIR), BF)],
-        ),
+        lambda *refs: inner_kernel(last, *refs),
+        out_shape=jax.ShapeDtypeStruct(slab.shape, BF),
+        in_specs=[SCALARS] + whole(4),
+        out_specs=ANYWHERE,
+        scratch_shapes=[
+            pltpu.VMEM((2, PAIR, PAIR), BF),
+            pltpu.VMEM(slab.shape, BF),
+            pltpu.SemaphoreType.DMA((2 * count + 1,)),
+        ],
         compiler_params=params(),
-        name="apply",
-    )(jnp.stack([core, position]).astype(jnp.int32), slab, own, other)
-
-
-def finish_kernel(last, idx_ref, before_ref, after_ref, part_ref, out_ref, sems):
+        name="inner",
+    )(numbers(core, position), slab, own, other, first)
+
+
+def place_kernel(last, idx_ref, block_ref, part_ref, out_ref, sem):
     del part_ref
-    position = idx_ref[0]
-
-    def low():
-        return pltpu.make_async_copy(before_ref, out_ref.at[:, pl.ds(0, B)], sems.at[0])
-
-    def high():
-        return pltpu.make_async_copy(after_ref, out_ref.at[:, pl.ds(PAIR + B, B)], sems.at[1])
-
-    @pl.when(position > 0)
-    def _():
-        low().start()
-
-    @pl.when(position < last)
-    def _():
-        high().start()
-
-    @pl.when(position > 0)
-    def _():
-        low().wait()
-
-    @pl.when(position < last)
-    def _():
-        high().wait()
-
-
-def finish(part, before, after, position, last):
-    anywhere = pl.BlockSpec(memory_space=pl.ANY)
+    core, position = idx_ref[0], idx_ref[1]
+    goes = ((core == 0) & (position > 0), (core == 1) & (position < last))
+    for side in range(2):
+
+        @pl.when(goes[side])
+        def _():
+            copy = pltpu.make_async_copy(
+                block_ref, out_ref.at[:, pl.ds(side * (PAIR + B), B)], sem.at[0]
+            )
+            copy.start()
+            copy.wait()
+
+
+def place(part, block, core, position, last):
     return pl.pallas_call(
-        lambda *refs: finish_kernel(last, *refs),
+        lambda *refs: place_kernel(last, *refs),
         out_shape=jax.ShapeDtypeStruct(part.shape, part.dtype),
-        grid_spec=pltpu.PrefetchScalarGridSpec(
-            num_scalar_prefetch=1,
-            grid=(1,),
-            in_specs=[anywhere] * 3,
-            out_specs=anywhere,
-            scratch_shapes=[pltpu.SemaphoreType.DMA((2,))],
-        ),
-        input_output_aliases={3: 0},
+        in_specs=[SCALARS] + whole(1) + [ANYWHERE],
+        out_specs=ANYWHERE,
+        scratch_shapes=[pltpu.SemaphoreType.DMA((1,))],
+        input_output_aliases={2: 0},
         compiler_params=params(),
-        name="finish",
-    )(position.reshape(1).astype(jnp.int32), before, after, part)
+        name="place",
+    )(numbers(core, position), block, part)
 
 
 def shifted(array, axis, by):
@@ -292,29 +346,56 @@
     return lax.ppermute(array, axis, [(i, (i + by) % size) for i in range(size)])
 
 
+def along_chain(array, ups):
+    size = lax.axis_size(("blk", "grp"))
+    moves = []
+    for core in range(2):
+        for i in range(size - 1):
+            pair = (core * size + i, core * size + i + 1)
+            moves.append(pair if core in ups else pair[::-1])
+    return lax.ppermute(array, ("core", "blk", "grp"), moves)
+
+
+def encode(chunk):
+    exponent = jnp.floor(jnp.log2(jnp.maximum(chunk[CHUNK : CHUNK + 1], 1e-30))) + 1.0
+    rows = lax.broadcasted_iota(jnp.int32, chunk.shape, 0)
+    scaled = chunk * jnp.exp2(TOP_EXPONENT - exponent)
+    return jnp.where(rows < CHUNK, scaled, exponent).astype(jnp.float16)
+
+
+def decode(message):
+    message = message.astype(F32)
+    exponent = message[CHUNK : CHUNK + 1]
+    rows = lax.broadcasted_iota(jnp.int32, message.shape, 0)
+    value = message * jnp.exp2(exponent - TOP_EXPONENT)
+    return jnp.where(rows < CHUNK, value, jnp.exp2(exponent))
+
+
 def body(slab):
     core, xi = lax.axis_index("core"), lax.axis_index("x")
     chain = ("blk", "grp")
-    size, position = lax.axis_size(chain), lax.axis_index(chain)
+    last, position = lax.axis_size(chain) - 1, lax.axis_index(chain)
 
     theirs = gram(slab, 1 - core, xi)
     received = shifted(theirs, "core", 1)
     packed = gram(slab, core, xi) + received
 
-    total = packed[:CHUNK]
-    parts = [
-        shifted(packed[i * CHUNK : (i + 1) * CHUNK], "x", i) for i in range(1, XS)
-    ]
-    total = total + parts[0] + parts[1] + parts[2]
-    total = total + shifted(total, "yh", 1)
-    chunks = [total] + [shifted(total, "x", i) for i in range(1, XS)]
+    total, *rest = (packed[i * SPAN : (i + 1) * SPAN] for i in range(XS))
+    parts = [shifted(encode(part), "x", i) for i, part in enumerate(rest, 1)]
+    for part in parts:
+        total = total + decode(part)
+    total = total + decode(shifted(encode(total), "yh", 1))
+    coded = encode(total)
+    chunks = [total] + [decode(shifted(coded, "x", i)) for i in range(1, XS)]
 
     own = rotation(chunks, xi)
+    first = edge(slab, own, core, 1 - core)
+    first = along_chain(first, (1,))
     other = shifted(own, "core", 1)
-    part, up, down = apply(slab, own, other, core, position)
-    before = lax.ppermute(up, chain, [(i, i + 1) for i in range(size - 1)])
-    after = lax.ppermute(down, chain, [(i, i - 1) for i in range(1, size)])
-    return finish(part, before, after, position, size - 1)
+    second = edge(slab, other, 1 - core, core)
+    second = along_chain(second, (0,))
+    out = inner(slab, own, other, first, core, position, last)
+    return place(out, second, core, position, last)
 
 
 def solution(mesh):

time: 74.4 us -> 68.5 us (0.921)
  waiting for transfers between devices: 33.1 us -> 19.7 us
  Pallas kernels: 20.2 us -> 23.7 us
  starting transfers between devices: 18.6 us -> 21.3 us
  other arithmetic: 0.35 us -> 1.38 us
    ppermute x9, waiting for transfers between devices: 21.4 us -> 10.9 us  [shifted(): lax.ppermute(array, axis, [(i, (i + by) % size) for i in range(size)])]
    pallas_call x4 -> x6, Pallas kernels: 9.12 us -> 12.6 us  [the longest x2 4.56 us: gram(): pl.pallas_call(gram_kernel, out_shape=jax.ShapeDtypeStruct((XS * SPAN, T)...]
    ppermute x9, starting transfers between devices: 10.7 us -> 13.5 us  [shifted(): lax.ppermute(array, axis, [(i, (i + by) % size) for i in range(size)])]
    ppermute x2, waiting for transfers between devices: 11.6 us -> 8.86 us  [along_chain(): return lax.ppermute(array, ('core', 'blk', 'grp'), moves)]
  transfers between devices with their start and end apart: 11 -> 11, of which waited for: 10 -> 8; matrix products, arithmetic and copies ran while one was open for 0% -> 1% of each run, Pallas kernels for 3% -> 12%
where the time goes in v2:
time: 68.5 us; the launch traced here: 67.9 us
  Pallas kernels  23.7 us (35%)
  starting transfers between devices  21.3 us (31%)
  waiting for transfers between devices  19.7 us (29%)
  local copies, waits for them, and re-layouts  1.59 us (2%)
  other arithmetic  1.38 us (2%)
    ppermute x9, starting transfers between devices, shifted(): lax.ppermute(array, axis, [(i, (i + by) % size) for i in range(size)])  13.5 us
    pallas_call x1, Pallas kernels, rotation(): pl.pallas_call(rotation_kernel, out_shape=jax.ShapeDtypeStruct((PAIR, PAI...  11.1 us
    ppermute x9, waiting for transfers between devices, shifted(): lax.ppermute(array, axis, [(i, (i + by) % size) for i in range(size)])  10.9 us
    ppermute x2, waiting for transfers between devices, along_chain(): return lax.ppermute(array, ('core', 'blk', 'grp'), moves)  8.86 us
    ppermute x2, starting transfers between devices, along_chain(): return lax.ppermute(array, ('core', 'blk', 'grp'), moves)  7.74 us
    pallas_call x2, Pallas kernels, gram(): pl.pallas_call(gram_kernel, out_shape=jax.ShapeDtypeStruct((XS * SPAN, T)...  4.56 us
    pallas_call x2, Pallas kernels, edge(): pl.pallas_call(edge_kernel, out_shape=jax.ShapeDtypeStruct((slab.shape[0]...  3.58 us
    pallas_call x1, Pallas kernels, inner(): pl.pallas_call(lambda *refs: inner_kernel(last, *refs), out_shape=jax.Sha...  2.62 us
  transfers between devices with their start and end apart: 11, of which 8 were waited for; matrix products, arithmetic and copies ran while one was open for 1% of the time, Pallas kernels for 12%

profile of v2, /device:TPU:8, one launch (start us, length us, event | category | flops | bytes accessed | tf_op | source)
XLA Modules:
  0.0 67.9 jit_solution(8310958810137920736)
XLA Ops:
  0.1 1.6 %copy-done = bf16[1024,1024]{1,0:T(8,128)(2,1)S(1)} copy-done((bf16[1024,1024]{1,0:T(8,128)(2,1)S(1)}, bf16[1024,1024]{1,0:T(8,128)(2,1)}, u32[]{:S(2)}) %copy-start) | copy-done | bytes 2097176
  1.7 2.3 %gram.3 = f32[1344,128]{1,0:T(8,128)S(1)} custom-call(s32[2]{0:T(128)S(1)} %pad_add_fusion.3.idx_ref, bf16[1024,1024]{1,0:T(8,128)(2,1)S(1)} %copy-done), custom_call_target="tpu_custom_call" | custom-call | tf_op jit(solution)/shard_map/gram/pallas_call | solution.py:88
  4.1 2.3 %gram.2 = f32[1344,128]{1,0:T(8,128)S(1)} custom-call(s32[2]{0:T(128)S(1)} %pad_add_fusion.4.idx_ref, bf16[1024,1024]{1,0:T(8,128)(2,1)S(1)} %copy-done.1), custom_call_target="tpu_custom_call" | custom-call | tf_op jit(solution)/shard_map/gram/pallas_call | solution.py:88
  6.7 3.1 %collective-permute-start.2 = (f16[336,128]{1,0:T(8,128)(2,1)S(1)}, f16[336,128]{1,0:T(8,128)(2,1)S(1)}, u32[]{:S(2)}, u32[]{:S(2)}) collective-permute-start(f16[336,128]{1,0:T(8,128)(2,1)S(1)} %get-tuple-element.17), channel_id=1, source_target_pairs={{0,32},{16,48},{32,0},{48,16},{1,33},{17,49},{33,1},{49,17},{2,34}... | collective-permute-start | bytes 258056 | tf_op jit(solution)/shard_map/ppermute | solution.py:346
  9.8 0.6 collective-permute-start.1
  10.4 2.6 %collective-permute-start.3 = (f16[336,128]{1,0:T(8,128)(2,1)S(1)}, f16[336,128]{1,0:T(8,128)(2,1)S(1)}, u32[]{:S(2)}, u32[]{:S(2)}) collective-permute-start(f16[336,128]{1,0:T(8,128)(2,1)S(1)} %get-tuple-element.16), channel_id=1, source_target_pairs={{0,48},{16,0},{32,16},{48,32},{1,49},{17,1},{33,17},{49,33},{2,50}... | collective-permute-start | bytes 258056 | tf_op jit(solution)/shard_map/ppermute | solution.py:346
  13.3 1.9 %collective-permute-done.3 = f16[336,128]{1,0:T(8,128)(2,1)S(1)} collective-permute-done((f16[336,128]{1,0:T(8,128)(2,1)S(1)}, f16[336,128]{1,0:T(8,128)(2,1)S(1)}, u32[]{:S(2)}, u32[]{:S(2)}) %collective-permute-start.3) | collective-permute-done | bytes 86048 | tf_op jit(solution)/shard_map/ppermute | solution.py:346
  15.2 0.5 collective-permute-done.1
  15.9 2.4 %collective-permute-start.4 = (f16[336,128]{1,0:T(8,128)(2,1)S(1)}, f16[336,128]{1,0:T(8,128)(2,1)S(1)}, u32[]{:S(2)}, u32[]{:S(2)}) collective-permute-start(f16[336,128]{1,0:T(8,128)(2,1)S(1)} %select_convert_fusion.1), channel_id=1, source_target_pairs={{0,64},{64,0},{1,65},{65,1},{2,66},{66,2},{3,67},{67,3},{4,68},{68... | collective-permute-start | bytes 258056 | tf_op jit(solution)/shard_map/ppermute | solution.py:346
  18.3 3.7 %collective-permute-done.4 = f16[336,128]{1,0:T(8,128)(2,1)S(1)} collective-permute-done((f16[336,128]{1,0:T(8,128)(2,1)S(1)}, f16[336,128]{1,0:T(8,128)(2,1)S(1)}, u32[]{:S(2)}, u32[]{:S(2)}) %collective-permute-start.4) | collective-permute-done | bytes 86048 | tf_op jit(solution)/shard_map/ppermute | solution.py:346
  22.3 1.0 %collective-permute-start.5 = (f16[336,128]{1,0:T(8,128)(2,1)S(1)}, f16[336,128]{1,0:T(8,128)(2,1)S(1)}, u32[]{:S(2)}, u32[]{:S(2)}) collective-permute-start(f16[336,128]{1,0:T(8,128)(2,1)S(1)} %select_convert_fusion), channel_id=1, source_target_pairs={{0,16},{16,32},{32,48},{48,0},{1,17},{17,33},{33,49},{49,1},{2,18}... | collective-permute-start | bytes 258056 | tf_op jit(solution)/shard_map/ppermute | solution.py:346
  23.3 2.3 %collective-permute-start.7 = (f16[336,128]{1,0:T(8,128)(2,1)S(1)}, f16[336,128]{1,0:T(8,128)(2,1)S(1)}, u32[]{:S(2)}, u32[]{:S(2)}) collective-permute-start(f16[336,128]{1,0:T(8,128)(2,1)S(1)} %select_convert_fusion), channel_id=1, source_target_pairs={{0,48},{16,0},{32,16},{48,32},{1,49},{17,1},{33,17},{49,33},{2,50}... | collective-permute-start | bytes 258056 | tf_op jit(solution)/shard_map/ppermute | solution.py:346
  25.6 1.3 %collective-permute-start.6 = (f16[336,128]{1,0:T(8,128)(2,1)S(1)}, f16[336,128]{1,0:T(8,128)(2,1)S(1)}, u32[]{:S(2)}, u32[]{:S(2)}) collective-permute-start(f16[336,128]{1,0:T(8,128)(2,1)S(1)} %select_convert_fusion), channel_id=1, source_target_pairs={{0,32},{16,48},{32,0},{48,16},{1,33},{17,49},{33,1},{49,17},{2,34}... | collective-permute-start | bytes 258056 | tf_op jit(solution)/shard_map/ppermute | solution.py:346
  27.0 2.0 %collective-permute-done.5 = f16[336,128]{1,0:T(8,128)(2,1)S(1)} collective-permute-done((f16[336,128]{1,0:T(8,128)(2,1)S(1)}, f16[336,128]{1,0:T(8,128)(2,1)S(1)}, u32[]{:S(2)}, u32[]{:S(2)}) %collective-permute-start.5) | collective-permute-done | bytes 86048 | tf_op jit(solution)/shard_map/ppermute | solution.py:346
  29.0 2.6 %collective-permute-done.6 = f16[336,128]{1,0:T(8,128)(2,1)S(1)} collective-permute-done((f16[336,128]{1,0:T(8,128)(2,1)S(1)}, f16[336,128]{1,0:T(8,128)(2,1)S(1)}, u32[]{:S(2)}, u32[]{:S(2)}) %collective-permute-start.6) | collective-permute-done | bytes 86048 | tf_op jit(solution)/shard_map/ppermute | solution.py:346
  31.8 11.1 %rotation.1.rot_ref.refs_2_ = bf16[512,512]{1,0:T(8,128)(2,1)S(1)} custom-call(s32[1]{0:T(128)} %bitcast.3.idx_ref, f32[336,128]{1,0:T(8,128)S(1)} %select_add_fusion.g0_ref, f32[336,128]{1,0:T(8,128)S(1)} %get-tuple-element.38.g1_ref, f32[336,128]{1,0:T(8,128)S(1)} %get-tuple-element.37.g2_ref, f32[336,128]{1,0:T(8,128)S(1)} %get-tuple-element.36.g3_ref), custom_call_target="tpu_custom_call" | custom-call | tf_op jit(solution)/shard_map/rotation/pallas_call | solution.py:185
  43.2 1.8 %edge.3 = bf16[1024,256]{1,0:T(8,128)(2,1)} custom-call(s32[2]{0:T(128)S(1)} %pad_add_fusion.2.idx_ref, bf16[1024,1024]{1,0:T(8,128)(2,1)S(1)} %copy-done.1, bf16[512,512]{1,0:T(8,128)(2,1)S(1)} %rotation.1.rot_ref.refs_2_), custom_call_target="tpu_custom_call" | custom-call | tf_op jit(solution)/shard_map/edge/pallas_call | solution.py:228
  45.0 5.8 %collective-permute-start.10 = (bf16[1024,256]{1,0:T(8,128)(2,1)}, bf16[1024,256]{1,0:T(8,128)(2,1)}, u32[]{:S(2)}, u32[]{:S(2)}) collective-permute-start(bf16[1024,256]{1,0:T(8,128)(2,1)} %edge.3), channel_id=1, source_target_pairs={{1,0},{2,1},{3,2},{4,3},{5,4},{6,5},{7,6},{8,9},{9,10},{10,11},{11... | collective-permute-start | bytes 1572872 | tf_op jit(solution)/shard_map/ppermute | solution.py:356
  50.8 1.8 %edge.2 = bf16[1024,256]{1,0:T(8,128)(2,1)} custom-call(s32[2]{0:T(128)S(1)} %pad_add_fusion.1.idx_ref, bf16[1024,1024]{1,0:T(8,128)(2,1)S(1)} %copy-done.1, bf16[512,512]{1,0:T(8,128)(2,1)S(1)} %collective-permute-done.8.rot_ref.refs_3_), custom_call_target="tpu_custom_call" | custom-call | tf_op jit(solution)/shard_map/edge/pallas_call | solution.py:228
  52.6 1.9 %collective-permute-start.9 = (bf16[1024,256]{1,0:T(8,128)(2,1)}, bf16[1024,256]{1,0:T(8,128)(2,1)}, u32[]{:S(2)}, u32[]{:S(2)}) collective-permute-start(bf16[1024,256]{1,0:T(8,128)(2,1)} %edge.2), channel_id=1, source_target_pairs={{0,1},{1,2},{2,3},{3,4},{4,5},{5,6},{6,7},{9,8},{10,9},{11,10},{12... | collective-permute-start | bytes 1572872 | tf_op jit(solution)/shard_map/ppermute | solution.py:356
  54.6 5.6 %collective-permute-done.10.refs_4_ = bf16[1024,256]{1,0:T(8,128)(2,1)} collective-permute-done((bf16[1024,256]{1,0:T(8,128)(2,1)}, bf16[1024,256]{1,0:T(8,128)(2,1)}, u32[]{:S(2)}, u32[]{:S(2)}) %collective-permute-start.10) | collective-permute-done | bytes 524320 | tf_op jit(solution)/shard_map/ppermute | solution.py:356
  60.2 2.6 %inner.1.refs_2_ = bf16[1024,1024]{1,0:T(8,128)(2,1)} custom-call(s32[2]{0:T(128)S(1)} %pad_add_fusion.refs_0_, bf16[1024,1024]{1,0:T(8,128)(2,1)S(1)} %copy-done.1, bf16[512,512]{1,0:T(8,128)(2,1)S(1)} %rotation.1.rot_ref.refs_2_, bf16[512,512]{1,0:T(8,128)(2,1)S(1)} %collective-permute-done.8.rot_ref.refs_3_, bf16[1024,256]{1,0:T(8,128)(2,1)} %collective-permute-done.10.refs_4_), custom_call_target="tpu_custom_call" | custom-call | tf_op jit(solution)/shard_map/inner/pallas_call | solution.py:301
  62.8 3.3 %collective-permute-done.9.refs_1_ = bf16[1024,256]{1,0:T(8,128)(2,1)} collective-permute-done((bf16[1024,256]{1,0:T(8,128)(2,1)}, bf16[1024,256]{1,0:T(8,128)(2,1)}, u32[]{:S(2)}, u32[]{:S(2)}) %collective-permute-start.9) | collective-permute-done | bytes 524320 | tf_op jit(solution)/shard_map/ppermute | solution.py:356
  66.1 1.9 %place.1 = bf16[1024,1024]{1,0:T(8,128)(2,1)} custom-call(s32[2]{0:T(128)S(1)} %pad_add_fusion.refs_0_, bf16[1024,256]{1,0:T(8,128)(2,1)} %collective-permute-done.9.refs_1_, bf16[1024,1024]{1,0:T(8,128)(2,1)} %inner.1.refs_2_), custom_call_target="tpu_custom_call", output_to_operand_aliasing={{}: (2, {})} | custom-call | tf_op jit(solution)/shard_map/place/pallas_call | solution.py:332
  (39 shorter events, 1.8 us)
Async XLA Ops:
  0.1 1.6 %copy-start = (bf16[1024,1024]{1,0:T(8,128)(2,1)S(1)}, bf16[1024,1024]{1,0:T(8,128)(2,1)}, u32[]{:S(2)}) copy-start(bf16[1024,1024]{1,0:T(8,128)(2,1)} %refs_1_.1) | copy-start | bytes 6291460
  1.7 2.5 %copy-start.1 = (bf16[1024,1024]{1,0:T(8,128)(2,1)S(1)}, bf16[1024,1024]{1,0:T(8,128)(2,1)}, u32[]{:S(2)}) copy-start(bf16[1024,1024]{1,0:T(8,128)(2,1)} %refs_1_.1) | copy-start | bytes 6291460
  4.0 2.5 %collective-permute-start = (f32[1344,128]{1,0:T(8,128)S(1)}, f32[1344,128]{1,0:T(8,128)S(1)}, u32[]{:S(2)}, u32[]{:S(2)}) collective-permute-start(f32[1344,128]{1,0:T(8,128)S(1)} %gram.3), channel_id=1, source_target_pairs={{0,8},{8,0},{1,9},{9,1},{2,10},{10,2},{3,11},{11,3},{4,12},{12,4},... | collective-permute-start | bytes 2064392 | tf_op jit(solution)/shard_map/ppermute | solution.py:346
  6.7 6.5 %collective-permute-start.2 = (f16[336,128]{1,0:T(8,128)(2,1)S(1)}, f16[336,128]{1,0:T(8,128)(2,1)S(1)}, u32[]{:S(2)}, u32[]{:S(2)}) collective-permute-start(f16[336,128]{1,0:T(8,128)(2,1)S(1)} %get-tuple-element.17), channel_id=1, source_target_pairs={{0,32},{16,48},{32,0},{48,16},{1,33},{17,49},{33,1},{49,17},{2,34}... | collective-permute-start | bytes 258056 | tf_op jit(solution)/shard_map/ppermute | solution.py:346
  9.8 5.9 %collective-permute-start.1 = (f16[336,128]{1,0:T(8,128)(2,1)S(1)}, f16[336,128]{1,0:T(8,128)(2,1)S(1)}, u32[]{:S(2)}, u32[]{:S(2)}) collective-permute-start(f16[336,128]{1,0:T(8,128)(2,1)S(1)} %get-tuple-element.15), channel_id=1, source_target_pairs={{0,16},{16,32},{32,48},{48,0},{1,17},{17,33},{33,49},{49,1},{2,18}... | collective-permute-start | bytes 258056 | tf_op jit(solution)/shard_map/ppermute | solution.py:346
  10.4 4.7 %collective-permute-start.3 = (f16[336,128]{1,0:T(8,128)(2,1)S(1)}, f16[336,128]{1,0:T(8,128)(2,1)S(1)}, u32[]{:S(2)}, u32[]{:S(2)}) collective-permute-start(f16[336,128]{1,0:T(8,128)(2,1)S(1)} %get-tuple-element.16), channel_id=1, source_target_pairs={{0,48},{16,0},{32,16},{48,32},{1,49},{17,1},{33,17},{49,33},{2,50}... | collective-permute-start | bytes 258056 | tf_op jit(solution)/shard_map/ppermute | solution.py:346
  15.9 6.1 %collective-permute-start.4 = (f16[336,128]{1,0:T(8,128)(2,1)S(1)}, f16[336,128]{1,0:T(8,128)(2,1)S(1)}, u32[]{:S(2)}, u32[]{:S(2)}) collective-permute-start(f16[336,128]{1,0:T(8,128)(2,1)S(1)} %select_convert_fusion.1), channel_id=1, source_target_pairs={{0,64},{64,0},{1,65},{65,1},{2,66},{66,2},{3,67},{67,3},{4,68},{68... | collective-permute-start | bytes 258056 | tf_op jit(solution)/shard_map/ppermute | solution.py:346
  22.3 6.7 %collective-permute-start.5 = (f16[336,128]{1,0:T(8,128)(2,1)S(1)}, f16[336,128]{1,0:T(8,128)(2,1)S(1)}, u32[]{:S(2)}, u32[]{:S(2)}) collective-permute-start(f16[336,128]{1,0:T(8,128)(2,1)S(1)} %select_convert_fusion), channel_id=1, source_target_pairs={{0,16},{16,32},{32,48},{48,0},{1,17},{17,33},{33,49},{49,1},{2,18}... | collective-permute-start | bytes 258056 | tf_op jit(solution)/shard_map/ppermute | solution.py:346
  23.3 8.3 %collective-permute-start.7 = (f16[336,128]{1,0:T(8,128)(2,1)S(1)}, f16[336,128]{1,0:T(8,128)(2,1)S(1)}, u32[]{:S(2)}, u32[]{:S(2)}) collective-permute-start(f16[336,128]{1,0:T(8,128)(2,1)S(1)} %select_convert_fusion), channel_id=1, source_target_pairs={{0,48},{16,0},{32,16},{48,32},{1,49},{17,1},{33,17},{49,33},{2,50}... | collective-permute-start | bytes 258056 | tf_op jit(solution)/shard_map/ppermute | solution.py:346
  25.6 6.0 %collective-permute-start.6 = (f16[336,128]{1,0:T(8,128)(2,1)S(1)}, f16[336,128]{1,0:T(8,128)(2,1)S(1)}, u32[]{:S(2)}, u32[]{:S(2)}) collective-permute-start(f16[336,128]{1,0:T(8,128)(2,1)S(1)} %select_convert_fusion), channel_id=1, source_target_pairs={{0,32},{16,48},{32,0},{48,16},{1,33},{17,49},{33,1},{49,17},{2,34}... | collective-permute-start | bytes 258056 | tf_op jit(solution)/shard_map/ppermute | solution.py:346
  42.9 7.9 %collective-permute-start.8 = (bf16[512,512]{1,0:T(8,128)(2,1)S(1)}, bf16[512,512]{1,0:T(8,128)(2,1)S(1)}, u32[]{:S(2)}, u32[]{:S(2)}) collective-permute-start(bf16[512,512]{1,0:T(8,128)(2,1)S(1)} %rotation.1.rot_ref.refs_2_), channel_id=1, source_target_pairs={{0,8},{8,0},{1,9},{9,1},{2,10},{10,2},{3,11},{11,3},{4,12},{12,4},... | collective-permute-start | bytes 1572872 | tf_op jit(solution)/shard_map/ppermute | solution.py:346
  45.0 15.2 %collective-permute-start.10 = (bf16[1024,256]{1,0:T(8,128)(2,1)}, bf16[1024,256]{1,0:T(8,128)(2,1)}, u32[]{:S(2)}, u32[]{:S(2)}) collective-permute-start(bf16[1024,256]{1,0:T(8,128)(2,1)} %edge.3), channel_id=1, source_target_pairs={{1,0},{2,1},{3,2},{4,3},{5,4},{6,5},{7,6},{8,9},{9,10},{10,11},{11... | collective-permute-start | bytes 1572872 | tf_op jit(solution)/shard_map/ppermute | solution.py:356
  52.6 13.5 %collective-permute-start.9 = (bf16[1024,256]{1,0:T(8,128)(2,1)}, bf16[1024,256]{1,0:T(8,128)(2,1)}, u32[]{:S(2)}, u32[]{:S(2)}) collective-permute-start(bf16[1024,256]{1,0:T(8,128)(2,1)} %edge.2), channel_id=1, source_target_pairs={{0,1},{1,2},{2,3},{3,4},{4,5},{5,6},{6,7},{9,8},{10,9},{11,10},{12... | collective-permute-start | bytes 1572872 | tf_op jit(solution)/shard_map/ppermute | solution.py:356

commit v3 on v2

--- a/solution.py
+++ b/solution.py
@@ -19,13 +19,13 @@
 SPAN = CHUNK + TAIL
 BF = jnp.bfloat16
 F32 = jnp.float32
-VMEM_LIMIT = 48 << 20
 ROW_TILE = 256
 TOP_EXPONENT = 14.0
-
-
-def params():
-    return pltpu.CompilerParams(vmem_limit_bytes=VMEM_LIMIT)
+ENOUGH = 2e-3
+
+
+def params(mib=8):
+    return pltpu.CompilerParams(vmem_limit_bytes=mib << 20)
 
 
 def dot(a, b):
@@ -42,90 +42,168 @@
 
 
 def mul(a, b):
-    return dot(a[0], b[0]) + (dot(a[0], b[1]) + dot(a[1], b[0]))
-
-
-def gram_kernel(idx_ref, a_ref, out_ref, acc_ref):
-    step = pl.program_id(0)
-    upper, lower = a_ref[:, :B], a_ref[:, B:]
-    pp, pq, qq = dot_tn(upper, upper), dot_tn(upper, lower), dot_tn(lower, lower)
-
-    @pl.when(step == 0)
-    def _():
-        acc_ref[0] = pp
-        acc_ref[1] = pq
-        acc_ref[2] = qq
-
-    @pl.when(step > 0)
-    def _():
-        acc_ref[0] += pp
-        acc_ref[1] += pq
-        acc_ref[2] += qq
-
-    @pl.when(step == pl.num_programs(0) - 1)
-    def _():
-        xi = idx_ref[1]
-        top = jnp.zeros((TAIL, T), F32)
-        for q in range(PACKED // PIECE):
-            row, col = BLOCKS[q * PIECE // T]
-            part = q * PIECE % T
-            which = row // 2 + col // 2
-            r0, c0 = row % 2 * T + part, col % 2 * T
-            chunk, offset = divmod(q * PIECE, CHUNK)
-            place = lax.rem(chunk - xi + XS, XS) * SPAN + offset
-            piece = acc_ref[which, r0 : r0 + PIECE, c0 : c0 + T]
-            out_ref[pl.ds(pl.multiple_of(place, TAIL), PIECE), :] = piece
-            for r in range(0, PIECE, TAIL):
-                top = jnp.maximum(top, jnp.abs(piece[r : r + TAIL]))
-        top = jnp.broadcast_to(jnp.max(top, axis=0, keepdims=True), (TAIL, T))
-        for i in range(XS):
-            out_ref[i * SPAN + CHUNK : (i + 1) * SPAN, :] = top
-
-
-def gram(slab, pair, xi):
-    rows = slab.shape[0]
-    tile = 256
-    return pl.pallas_call(
-        gram_kernel,
-        out_shape=jax.ShapeDtypeStruct((XS * SPAN, T), F32),
-        grid_spec=pltpu.PrefetchScalarGridSpec(
-            num_scalar_prefetch=1,
-            grid=(rows // tile,),
-            in_specs=[pl.BlockSpec((tile, PAIR), lambda i, idx: (i, idx[0]))],
-            out_specs=pl.BlockSpec((XS * SPAN, T), lambda i, idx: (0, 0)),
-            scratch_shapes=[pltpu.VMEM((3, B, B), F32)],
+    left = jnp.concatenate([a[0], a[0], a[1]], axis=1)
+    return dot(left, jnp.concatenate([b[0], b[1], b[0]], axis=0))
+
+
+def whole(count):
+    return [pl.BlockSpec(memory_space=pltpu.VMEM)] * count
+
+
+def numbers(*values):
+    return jnp.stack(values).astype(jnp.int32)
+
+
+SCALARS = pl.BlockSpec(memory_space=pltpu.SMEM)
+ANYWHERE = pl.BlockSpec(memory_space=pl.ANY)
+
+
+def row_tiles(rows):
+    return [pl.ds(i * ROW_TILE, ROW_TILE) for i in range(rows // ROW_TILE)]
+
+
+def pack(acc, xi, out_ref):
+    top = jnp.zeros((TAIL, T), F32)
+    for q in range(PACKED // PIECE):
+        row, col = BLOCKS[q * PIECE // T]
+        part = q * PIECE % T
+        which = row // 2 + col // 2
+        r0, c0 = row % 2 * T + part, col % 2 * T
+        chunk, offset = divmod(q * PIECE, CHUNK)
+        place = lax.rem(chunk - xi + XS, XS) * SPAN + offset
+        piece = acc[which][r0 : r0 + PIECE, c0 : c0 + T]
+        out_ref[pl.ds(pl.multiple_of(place, TAIL), PIECE), :] = piece
+        for r in range(0, PIECE, TAIL):
+            top = jnp.maximum(top, jnp.abs(piece[r : r + TAIL]))
+    top = jnp.broadcast_to(jnp.max(top, axis=0, keepdims=True), (TAIL, T))
+    for i in range(XS):
+        out_ref[i * SPAN + CHUNK : (i + 1) * SPAN, :] = top
+
+
+def products(rows):
+    upper, lower = rows[:, :B], rows[:, B:]
+    return dot_tn(upper, upper), dot_tn(upper, lower), dot_tn(lower, lower)
+
+
+def first_gram_kernel(idx_ref, a_ref, out_ref, slab_ref, sems):
+    pair, xi = idx_ref[0], idx_ref[1]
+    tiles = row_tiles(a_ref.shape[0])
+
+    def fetch(which, i):
+        columns = pl.ds(pl.multiple_of(which * PAIR, PAIR), PAIR)
+        return pltpu.make_async_copy(
+            a_ref.at[tiles[i], columns], slab_ref.at[tiles[i], columns], sems.at[i]
+        )
+
+    def fetch_other(i):
+        columns = pl.ds(pl.multiple_of((1 - pair) * PAIR, PAIR), PAIR)
+        return pltpu.make_async_copy(
+            a_ref.at[tiles[i], columns],
+            slab_ref.at[tiles[i], columns],
+            sems.at[len(tiles) + i],
+        )
+
+    for i in range(len(tiles)):
+        fetch(pair, i).start()
+    for i in range(len(tiles)):
+        fetch_other(i).start()
+    columns = pl.ds(pl.multiple_of(pair * PAIR, PAIR), PAIR)
+    total = None
+    for i, tile in enumerate(tiles):
+        fetch(pair, i).wait()
+        new = products(slab_ref[tile, columns])
+        total = new if total is None else [x + y for x, y in zip(total, new)]
+    pack(total, xi, out_ref)
+    for i in range(len(tiles)):
+        fetch_other(i).wait()
+
+
+def first_gram(slab, pair, xi):
+    count = slab.shape[0] // ROW_TILE
+    return pl.pallas_call(
+        first_gram_kernel,
+        out_shape=(
+            pltpu.VMEM((XS * SPAN, T), F32),
+            pltpu.VMEM(slab.shape, slab.dtype),
         ),
+        in_specs=[SCALARS, pl.BlockSpec(memory_space=pltpu.HBM)],
+        out_specs=tuple(whole(2)),
+        scratch_shapes=[pltpu.SemaphoreType.DMA((2 * count,))],
         compiler_params=params(),
-        name="gram",
-    )(jnp.stack([pair, xi]).astype(jnp.int32), slab)
+        name="first_gram",
+    )(numbers(pair, xi), pltpu.with_memory_space_constraint(slab, pltpu.HBM))
+
+
+def second_gram_kernel(idx_ref, slab_ref, out_ref):
+    columns = pl.ds(pl.multiple_of(idx_ref[0] * PAIR, PAIR), PAIR)
+    total = None
+    for tile in row_tiles(slab_ref.shape[0]):
+        new = products(slab_ref[tile, columns])
+        total = new if total is None else [x + y for x, y in zip(total, new)]
+    pack(total, idx_ref[1], out_ref)
+
+
+def second_gram(slab, pair, xi):
+    return pl.pallas_call(
+        second_gram_kernel,
+        out_shape=pltpu.VMEM((XS * SPAN, T), F32),
+        in_specs=[SCALARS] + whole(1),
+        out_specs=whole(1)[0],
+        compiler_params=params(),
+        name="second_gram",
+    )(numbers(pair, xi), slab)
 
 
 def inverse(gramian, eye):
     top = jnp.sqrt(jnp.sum(gramian * gramian))
     scale = 2.0 / (2.0 + top)
-    gap = scale
     rest = eye - scale * (eye + gramian)
+
+    def rates(gap):
+        rate = 1.0 - gap
+        grown = 2.0 * gap * (2.0 - gap) / (1.0 + gap * (2.0 - gap))
+        return 2.0 / (2.0 - rate * rate), grown
 
     def more(state):
         count, gap, _, _ = state
-        return (gap < 1.0 - 1e-6) & (count < 60)
+        return (gap < 1.0 - ENOUGH) & (count < 60)
 
     def step(state):
         count, gap, rest, approx = state
-        rate = 1.0 - gap
-        c = 2.0 / (2.0 - rate * rate)
+        c, gap = rates(gap)
         parts = split(rest)
         square = mul(parts, parts)
         approx = c * (approx + mul(split(approx), parts))
-        rest = c * square + (1.0 - c) * eye
-        gap = 2.0 * gap * (2.0 - gap) / (1.0 + gap * (2.0 - gap))
-        return count + 1, gap, rest, approx
-
-    state = (jnp.int32(0), gap, rest, scale * eye)
-    return lax.while_loop(more, step, state)[3]
-
-
-def rotation_kernel(idx_ref, g0_ref, g1_ref, g2_ref, g3_ref, out_ref, pack_ref, h_ref, e_ref):
+        return count + 1, gap, c * square + (1.0 - c) * eye, approx
+
+    c, gap = rates(scale)
+    parts = split(rest)
+    approx = (c * scale) * (eye + rest)
+    rest = c * mul(parts, parts) + (1.0 - c) * eye
+    _, gap, rest, approx = lax.while_loop(more, step, (jnp.int32(0), gap, rest, approx))
+    c, _ = rates(gap)
+    return c * (approx + mul(split(approx), split(rest)))
+
+
+def turn(parts):
+    return parts[0].T, parts[1].T
+
+
+def side_by_side(blocks):
+    return jnp.concatenate([jnp.concatenate(row, axis=1) for row in blocks], axis=0)
+
+
+def stacked(blocks):
+    return tuple(side_by_side([[b[i] for b in row] for row in blocks]) for i in range(2))
+
+
+def negative(parts):
+    return -parts[0], -parts[1]
+
+
+def rotation_kernel(
+    idx_ref, g0_ref, g1_ref, g2_ref, g3_ref, out_ref, pack_ref, h_ref, e_ref
+):
     xi = idx_ref[0]
     for i, ref in enumerate((g0_ref, g1_ref, g2_ref, g3_ref)):
         place = lax.rem(xi - i + XS, XS) * CHUNK
@@ -138,46 +216,41 @@
     rows = lax.broadcasted_iota(jnp.int32, (B, B), 0)
     cols = lax.broadcasted_iota(jnp.int32, (B, B), 1)
     eye = jnp.where(rows == cols, 1.0, 0.0).astype(F32)
+    hpp, hpq, hqq = h_ref[:B, :B], h_ref[:B, B:], h_ref[B:, B:]
 
     for sweep in range(INNER):
-        trace = jnp.sum((h_ref[:B, :B] + h_ref[B:, B:]) * eye)
+        trace = jnp.sum((hpp + hqq) * eye)
         mean = trace / PAIR + 1e-6
         factor = -1.0 / (mean * mean)
-        pp, pq = split(h_ref[:B, :B]), split(h_ref[:B, B:])
-        qp, qq = split(h_ref[B:, :B]), split(h_ref[B:, B:])
-        x = split((mul(pp, pq) - mul(pq, qq)) * factor)
-        xt = split((mul(qp, pp) - mul(qq, qp)) * factor)
+        pq = split(hpq)
+        x = split((mul(split(hpp), pq) - mul(pq, split(hqq))) * factor)
+        xt = turn(x)
         pi = inverse(mul(x, xt), eye)
-        pis = split(pi)
-        w = mul(pis, x)
-        wt = mul(xt, pis)
-        t = mul(split(wt), x)
-        e = jnp.concatenate(
-            [
-                jnp.concatenate([2.0 * (pi - eye), 2.0 * w], axis=1),
-                jnp.concatenate([-2.0 * wt, -2.0 * t], axis=1),
-            ],
-            axis=0,
-        )
-        if sweep == 0:
-            e_ref[...] = e
-            et = jnp.concatenate(
-                [
-                    jnp.concatenate([2.0 * (pi - eye), -2.0 * w], axis=1),
-                    jnp.concatenate([2.0 * wt, -2.0 * t], axis=1),
-                ],
-                axis=0,
-            )
+        w = mul(split(pi), x)
+        ws = split(2.0 * w)
+        wt = turn(ws)
+        corner = split(2.0 * (pi - eye))
+        t = split(mul(xt, negative(ws)))
+        e = stacked([[corner, ws], [negative(wt), t]])
+        if sweep + 1 < INNER:
             h = h_ref[...]
-            m = h + mul(split(h), split(e))
-            h_ref[...] = m + mul(split(et), split(m))
+            m = h + mul(split(h), e)
+            left, right = split(m[:, :B]), split(m[:, B:])
+            low = stacked([[corner, negative(ws)]])
+            high = stacked([[wt, t]])
+            hpp = m[:B, :B] + mul(low, left)
+            hpq = m[:B, B:] + mul(low, right)
+            hqq = m[B:, B:] + mul(high, right)
+            for i in range(2):
+                e_ref[i] = e[i]
         else:
-            first = e_ref[...]
+            first = e_ref[0], e_ref[1]
+            plain = first[0].astype(F32) + first[1].astype(F32)
+            both = e[0].astype(F32) + e[1].astype(F32)
             r = lax.broadcasted_iota(jnp.int32, (PAIR, PAIR), 0)
             c = lax.broadcasted_iota(jnp.int32, (PAIR, PAIR), 1)
-            whole = jnp.where(r == c, 1.0, 0.0).astype(F32)
-            v = whole + (first + e) + mul(split(first), split(e))
-            out_ref[...] = v.astype(BF)
+            unit = jnp.where(r == c, 1.0, 0.0).astype(F32)
+            out_ref[...] = (unit + (plain + both) + mul(first, e)).astype(BF)
 
 
 def rotation(chunks, xi):
@@ -193,28 +266,12 @@
             scratch_shapes=[
                 pltpu.VMEM((PACKED, T), F32),
                 pltpu.VMEM((PAIR, PAIR), F32),
-                pltpu.VMEM((PAIR, PAIR), F32),
+                pltpu.VMEM((2, PAIR, PAIR), BF),
             ],
         ),
-        compiler_params=params(),
+        compiler_params=params(24),
         name="rotation",
     )(xi.reshape(1).astype(jnp.int32), *chunks)
-
-
-def whole(count):
-    return [pl.BlockSpec(memory_space=pltpu.VMEM)] * count
-
-
-def numbers(*values):
-    return jnp.stack(values).astype(jnp.int32)
-
-
-SCALARS = pl.BlockSpec(memory_space=pltpu.SMEM)
-ANYWHERE = pl.BlockSpec(memory_space=pl.ANY)
-
-
-def row_tiles(rows):
-    return [pl.ds(i * ROW_TILE, ROW_TILE) for i in range(rows // ROW_TILE)]
 
 
 def edge_kernel(idx_ref, a_ref, rot_ref, out_ref):
@@ -227,7 +284,7 @@
 def edge(slab, rot, pair, half):
     return pl.pallas_call(
         edge_kernel,
-        out_shape=jax.ShapeDtypeStruct((slab.shape[0], B), BF),
+        out_shape=pltpu.VMEM((slab.shape[0], B), BF),
         in_specs=[SCALARS] + whole(2),
         out_specs=whole(1)[0],
         compiler_params=params(),
@@ -376,9 +433,9 @@
     chain = ("blk", "grp")
     last, position = lax.axis_size(chain) - 1, lax.axis_index(chain)
 
-    theirs = gram(slab, 1 - core, xi)
+    theirs, slab = first_gram(slab, 1 - core, xi)
     received = shifted(theirs, "core", 1)
-    packed = gram(slab, core, xi) + received
+    packed = second_gram(slab, core, xi) + received
 
     total, *rest = (packed[i * SPAN : (i + 1) * SPAN] for i in range(XS))
     parts = [shifted(encode(part), "x", i) for i, part in enumerate(rest, 1)]

time: 68.5 us -> 66.2 us (0.966)
  waiting for transfers between devices: 19.7 us -> 21.9 us
  Pallas kernels: 23.7 us -> 22.1 us
  local copies, waits for them, and re-layouts: 1.59 us -> 0 us
  starting transfers between devices: 21.3 us -> 20 us
    ppermute x9, waiting for transfers between devices: 10.9 us -> 13 us  [shifted(): lax.ppermute(array, axis, [(i, (i + by) % size) for i in range(size)])]
    unnamed x4 -> x0, local copies, waits for them, and re-layouts: 1.59 us -> none
    ppermute x9, starting transfers between devices: 13.5 us -> 12.3 us  [shifted(): lax.ppermute(array, axis, [(i, (i + by) % size) for i in range(size)])]
    pallas_call x1, Pallas kernels: 11.1 us -> 10.2 us  [rotation(): pl.pallas_call(rotation_kernel, out_shape=jax.ShapeDtypeStruct((PAIR, PAI...]
    pallas_call x4, Pallas kernels: 8.13 us -> 7.39 us  [the longest x2 3.57 us: edge(): pl.pallas_call(edge_kernel, out_shape=pltpu.VMEM((slab.shape[0], B), BF),...]
  transfers between devices with their start and end apart: 11 -> 11, of which waited for: 8 -> 10; matrix products, arithmetic and copies ran while one was open for 1% -> 1% of each run, Pallas kernels for 12% -> 11%
where the time goes in v3:
time: 66.2 us; the launch traced here: 65.6 us
  Pallas kernels  22.1 us (33%)
  waiting for transfers between devices  21.9 us (33%)
  starting transfers between devices  20 us (30%)
  other arithmetic  1.37 us (2%)
    ppermute x9, waiting for transfers between devices, shifted(): lax.ppermute(array, axis, [(i, (i + by) % size) for i in range(size)])  13 us
    ppermute x9, starting transfers between devices, shifted(): lax.ppermute(array, axis, [(i, (i + by) % size) for i in range(size)])  12.3 us
    pallas_call x1, Pallas kernels, rotation(): pl.pallas_call(rotation_kernel, out_shape=jax.ShapeDtypeStruct((PAIR, PAI...  10.2 us
    ppermute x2, waiting for transfers between devices, along_chain(): return lax.ppermute(array, ('core', 'blk', 'grp'), moves)  8.86 us
    ppermute x2, starting transfers between devices, along_chain(): return lax.ppermute(array, ('core', 'blk', 'grp'), moves)  7.73 us
    pallas_call x2, Pallas kernels, edge(): pl.pallas_call(edge_kernel, out_shape=pltpu.VMEM((slab.shape[0], B), BF),...  3.57 us
    pallas_call x1, Pallas kernels, inner(): pl.pallas_call(lambda *refs: inner_kernel(last, *refs), out_shape=jax.Sha...  2.62 us
    pallas_call x1, Pallas kernels, first_gram(): pl.pallas_call(first_gram_kernel, out_shape=(pltpu.VMEM((XS * SPAN, T), F...  2.6 us
  transfers between devices with their start and end apart: 11, of which 10 were waited for; matrix products, arithmetic and copies ran while one was open for 1% of the time, Pallas kernels for 11%

profile of v3, /device:TPU:8, one launch (start us, length us, event | category | flops | bytes accessed | tf_op | source)
XLA Modules:
  0.0 65.6 jit_solution(18345834988411552525)
XLA Ops:
  0.1 2.6 %first_gram.1 = (f32[1344,128]{1,0:T(8,128)S(1)}, bf16[1024,1024]{1,0:T(8,128)(2,1)S(1)}) custom-call(s32[2]{0:T(128)S(1)} %pad_add_fusion.3.idx_ref, bf16[1024,1024]{1,0:T(8,128)(2,1)} %a_ref.1), custom_call_target="tpu_custom_call" | custom-call | tf_op jit(solution)/shard_map/first_gram/pallas_call | solution.py:123
  2.9 1.2 %second_gram.1 = f32[1344,128]{1,0:T(8,128)S(1)} custom-call(s32[2]{0:T(128)S(1)} %pad_add_fusion.4.idx_ref, bf16[1024,1024]{1,0:T(8,128)(2,1)S(1)} %get-tuple-element.7.slab_ref.a_ref.refs_1_), custom_call_target="tpu_custom_call" | custom-call | tf_op jit(solution)/shard_map/second_gram/pallas_call | solution.py:147
  4.1 0.8 %collective-permute-done = f32[1344,128]{1,0:T(8,128)S(1)} collective-permute-done((f32[1344,128]{1,0:T(8,128)S(1)}, f32[1344,128]{1,0:T(8,128)S(1)}, u32[]{:S(2)}, u32[]{:S(2)}) %collective-permute-start) | collective-permute-done | bytes 688160 | tf_op jit(solution)/shard_map/ppermute | solution.py:403
  5.1 1.6 %collective-permute-start.1 = (f16[336,128]{1,0:T(8,128)(2,1)S(1)}, f16[336,128]{1,0:T(8,128)(2,1)S(1)}, u32[]{:S(2)}, u32[]{:S(2)}) collective-permute-start(f16[336,128]{1,0:T(8,128)(2,1)S(1)} %get-tuple-element.19), channel_id=1, source_target_pairs={{0,16},{16,32},{32,48},{48,0},{1,17},{17,33},{33,49},{49,1},{2,18}... | collective-permute-start | bytes 258056 | tf_op jit(solution)/shard_map/ppermute | solution.py:403
  6.7 2.7 %collective-permute-start.2 = (f16[336,128]{1,0:T(8,128)(2,1)S(1)}, f16[336,128]{1,0:T(8,128)(2,1)S(1)}, u32[]{:S(2)}, u32[]{:S(2)}) collective-permute-start(f16[336,128]{1,0:T(8,128)(2,1)S(1)} %get-tuple-element.21), channel_id=1, source_target_pairs={{0,32},{16,48},{32,0},{48,16},{1,33},{17,49},{33,1},{49,17},{2,34}... | collective-permute-start | bytes 258056 | tf_op jit(solution)/shard_map/ppermute | solution.py:403
  9.4 1.4 %collective-permute-start.3 = (f16[336,128]{1,0:T(8,128)(2,1)S(1)}, f16[336,128]{1,0:T(8,128)(2,1)S(1)}, u32[]{:S(2)}, u32[]{:S(2)}) collective-permute-start(f16[336,128]{1,0:T(8,128)(2,1)S(1)} %get-tuple-element.20), channel_id=1, source_target_pairs={{0,48},{16,0},{32,16},{48,32},{1,49},{17,1},{33,17},{49,33},{2,50}... | collective-permute-start | bytes 258056 | tf_op jit(solution)/shard_map/ppermute | solution.py:403
  11.0 2.8 %collective-permute-done.2 = f16[336,128]{1,0:T(8,128)(2,1)S(1)} collective-permute-done((f16[336,128]{1,0:T(8,128)(2,1)S(1)}, f16[336,128]{1,0:T(8,128)(2,1)S(1)}, u32[]{:S(2)}, u32[]{:S(2)}) %collective-permute-start.2) | collective-permute-done | bytes 86048 | tf_op jit(solution)/shard_map/ppermute | solution.py:403
  14.2 2.4 %collective-permute-start.4 = (f16[336,128]{1,0:T(8,128)(2,1)S(1)}, f16[336,128]{1,0:T(8,128)(2,1)S(1)}, u32[]{:S(2)}, u32[]{:S(2)}) collective-permute-start(f16[336,128]{1,0:T(8,128)(2,1)S(1)} %select_convert_fusion.1), channel_id=1, source_target_pairs={{0,64},{64,0},{1,65},{65,1},{2,66},{66,2},{3,67},{67,3},{4,68},{68... | collective-permute-start | bytes 258056 | tf_op jit(solution)/shard_map/ppermute | solution.py:403
  16.6 3.7 %collective-permute-done.4 = f16[336,128]{1,0:T(8,128)(2,1)S(1)} collective-permute-done((f16[336,128]{1,0:T(8,128)(2,1)S(1)}, f16[336,128]{1,0:T(8,128)(2,1)S(1)}, u32[]{:S(2)}, u32[]{:S(2)}) %collective-permute-start.4) | collective-permute-done | bytes 86048 | tf_op jit(solution)/shard_map/ppermute | solution.py:403
  20.6 2.7 %collective-permute-start.7 = (f16[336,128]{1,0:T(8,128)(2,1)S(1)}, f16[336,128]{1,0:T(8,128)(2,1)S(1)}, u32[]{:S(2)}, u32[]{:S(2)}) collective-permute-start(f16[336,128]{1,0:T(8,128)(2,1)S(1)} %select_convert_fusion), channel_id=1, source_target_pairs={{0,48},{16,0},{32,16},{48,32},{1,49},{17,1},{33,17},{49,33},{2,50}... | collective-permute-start | bytes 258056 | tf_op jit(solution)/shard_map/ppermute | solution.py:403
  23.3 0.7 %collective-permute-start.6 = (f16[336,128]{1,0:T(8,128)(2,1)S(1)}, f16[336,128]{1,0:T(8,128)(2,1)S(1)}, u32[]{:S(2)}, u32[]{:S(2)}) collective-permute-start(f16[336,128]{1,0:T(8,128)(2,1)S(1)} %select_convert_fusion), channel_id=1, source_target_pairs={{0,32},{16,48},{32,0},{48,16},{1,33},{17,49},{33,1},{49,17},{2,34}... | collective-permute-start | bytes 258056 | tf_op jit(solution)/shard_map/ppermute | solution.py:403
  24.0 0.6 collective-permute-start.5
  24.6 0.8 %collective-permute-done.7 = f16[336,128]{1,0:T(8,128)(2,1)S(1)} collective-permute-done((f16[336,128]{1,0:T(8,128)(2,1)S(1)}, f16[336,128]{1,0:T(8,128)(2,1)S(1)}, u32[]{:S(2)}, u32[]{:S(2)}) %collective-permute-start.7) | collective-permute-done | bytes 86048 | tf_op jit(solution)/shard_map/ppermute | solution.py:403
  25.4 3.9 %collective-permute-done.6 = f16[336,128]{1,0:T(8,128)(2,1)S(1)} collective-permute-done((f16[336,128]{1,0:T(8,128)(2,1)S(1)}, f16[336,128]{1,0:T(8,128)(2,1)S(1)}, u32[]{:S(2)}, u32[]{:S(2)}) %collective-permute-start.6) | collective-permute-done | bytes 86048 | tf_op jit(solution)/shard_map/ppermute | solution.py:403
  29.4 0.8 %collective-permute-done.5 = f16[336,128]{1,0:T(8,128)(2,1)S(1)} collective-permute-done((f16[336,128]{1,0:T(8,128)(2,1)S(1)}, f16[336,128]{1,0:T(8,128)(2,1)S(1)}, u32[]{:S(2)}, u32[]{:S(2)}) %collective-permute-start.5) | collective-permute-done | bytes 86048 | tf_op jit(solution)/shard_map/ppermute | solution.py:403
  30.4 10.2 %rotation.1.rot_ref.refs_2_ = bf16[512,512]{1,0:T(8,128)(2,1)S(1)} custom-call(s32[1]{0:T(128)} %bitcast.3.idx_ref, f32[336,128]{1,0:T(8,128)S(1)} %select_add_fusion.g0_ref, f32[336,128]{1,0:T(8,128)S(1)} %get-tuple-element.42.g1_ref, f32[336,128]{1,0:T(8,128)S(1)} %get-tuple-element.41.g2_ref, f32[336,128]{1,0:T(8,128)S(1)} %get-tuple-element.40.g3_ref), custom_call_target="tpu_custom_call" | custom-call | tf_op jit(solution)/shard_map/rotation/pallas_call | solution.py:258
  40.9 1.8 %edge.3 = bf16[1024,256]{1,0:T(8,128)(2,1)} custom-call(s32[2]{0:T(128)S(1)} %pad_add_fusion.2.idx_ref, bf16[1024,1024]{1,0:T(8,128)(2,1)S(1)} %get-tuple-element.7.slab_ref.a_ref.refs_1_, bf16[512,512]{1,0:T(8,128)(2,1)S(1)} %rotation.1.rot_ref.refs_2_), custom_call_target="tpu_custom_call" | custom-call | tf_op jit(solution)/shard_map/edge/pallas_call | solution.py:285
  42.7 5.8 %collective-permute-start.10 = (bf16[1024,256]{1,0:T(8,128)(2,1)}, bf16[1024,256]{1,0:T(8,128)(2,1)}, u32[]{:S(2)}, u32[]{:S(2)}) collective-permute-start(bf16[1024,256]{1,0:T(8,128)(2,1)} %edge.3), channel_id=1, source_target_pairs={{1,0},{2,1},{3,2},{4,3},{5,4},{6,5},{7,6},{8,9},{9,10},{10,11},{11... | collective-permute-start | bytes 1572872 | tf_op jit(solution)/shard_map/ppermute | solution.py:413
  48.5 1.8 %edge.2 = bf16[1024,256]{1,0:T(8,128)(2,1)} custom-call(s32[2]{0:T(128)S(1)} %pad_add_fusion.1.idx_ref, bf16[1024,1024]{1,0:T(8,128)(2,1)S(1)} %get-tuple-element.7.slab_ref.a_ref.refs_1_, bf16[512,512]{1,0:T(8,128)(2,1)S(1)} %collective-permute-done.8.rot_ref.refs_3_), custom_call_target="tpu_custom_call" | custom-call | tf_op jit(solution)/shard_map/edge/pallas_call | solution.py:285
  50.3 1.9 %collective-permute-start.9 = (bf16[1024,256]{1,0:T(8,128)(2,1)}, bf16[1024,256]{1,0:T(8,128)(2,1)}, u32[]{:S(2)}, u32[]{:S(2)}) collective-permute-start(bf16[1024,256]{1,0:T(8,128)(2,1)} %edge.2), channel_id=1, source_target_pairs={{0,1},{1,2},{2,3},{3,4},{4,5},{5,6},{6,7},{9,8},{10,9},{11,10},{12... | collective-permute-start | bytes 1572872 | tf_op jit(solution)/shard_map/ppermute | solution.py:413
  52.3 5.6 %collective-permute-done.10.refs_4_ = bf16[1024,256]{1,0:T(8,128)(2,1)} collective-permute-done((bf16[1024,256]{1,0:T(8,128)(2,1)}, bf16[1024,256]{1,0:T(8,128)(2,1)}, u32[]{:S(2)}, u32[]{:S(2)}) %collective-permute-start.10) | collective-permute-done | bytes 524320 | tf_op jit(solution)/shard_map/ppermute | solution.py:413
  57.9 2.6 %inner.1.refs_2_ = bf16[1024,1024]{1,0:T(8,128)(2,1)} custom-call(s32[2]{0:T(128)S(1)} %pad_add_fusion.refs_0_, bf16[1024,1024]{1,0:T(8,128)(2,1)S(1)} %get-tuple-element.7.slab_ref.a_ref.refs_1_, bf16[512,512]{1,0:T(8,128)(2,1)S(1)} %rotation.1.rot_ref.refs_2_, bf16[512,512]{1,0:T(8,128)(2,1)S(1)} %collective-permute-done.8.rot_ref.refs_3_, ...), custom_call_target="tpu_custom_call" | custom-call | tf_op jit(solution)/shard_map/inner/pallas_call | solution.py:358
  60.5 3.3 %collective-permute-done.9.refs_1_ = bf16[1024,256]{1,0:T(8,128)(2,1)} collective-permute-done((bf16[1024,256]{1,0:T(8,128)(2,1)}, bf16[1024,256]{1,0:T(8,128)(2,1)}, u32[]{:S(2)}, u32[]{:S(2)}) %collective-permute-start.9) | collective-permute-done | bytes 524320 | tf_op jit(solution)/shard_map/ppermute | solution.py:413
  63.8 1.9 %place.1 = bf16[1024,1024]{1,0:T(8,128)(2,1)} custom-call(s32[2]{0:T(128)S(1)} %pad_add_fusion.refs_0_, bf16[1024,256]{1,0:T(8,128)(2,1)} %collective-permute-done.9.refs_1_, bf16[1024,1024]{1,0:T(8,128)(2,1)} %inner.1.refs_2_), custom_call_target="tpu_custom_call", output_to_operand_aliasing={{}: (2, {})} | custom-call | tf_op jit(solution)/shard_map/place/pallas_call | solution.py:389
  (35 shorter events, 1.7 us)
Async XLA Ops:
  2.7 2.2 %collective-permute-start = (f32[1344,128]{1,0:T(8,128)S(1)}, f32[1344,128]{1,0:T(8,128)S(1)}, u32[]{:S(2)}, u32[]{:S(2)}) collective-permute-start(f32[1344,128]{1,0:T(8,128)S(1)} %get-tuple-element.8), channel_id=1, source_target_pairs={{0,8},{8,0},{1,9},{9,1},{2,10},{10,2},{3,11},{11,3},{4,12},{12,4},... | collective-permute-start | bytes 2064392 | tf_op jit(solution)/shard_map/ppermute | solution.py:403
  5.1 5.9 %collective-permute-start.1 = (f16[336,128]{1,0:T(8,128)(2,1)S(1)}, f16[336,128]{1,0:T(8,128)(2,1)S(1)}, u32[]{:S(2)}, u32[]{:S(2)}) collective-permute-start(f16[336,128]{1,0:T(8,128)(2,1)S(1)} %get-tuple-element.19), channel_id=1, source_target_pairs={{0,16},{16,32},{32,48},{48,0},{1,17},{17,33},{33,49},{49,1},{2,18}... | collective-permute-start | bytes 258056 | tf_op jit(solution)/shard_map/ppermute | solution.py:403
  6.7 7.1 %collective-permute-start.2 = (f16[336,128]{1,0:T(8,128)(2,1)S(1)}, f16[336,128]{1,0:T(8,128)(2,1)S(1)}, u32[]{:S(2)}, u32[]{:S(2)}) collective-permute-start(f16[336,128]{1,0:T(8,128)(2,1)S(1)} %get-tuple-element.21), channel_id=1, source_target_pairs={{0,32},{16,48},{32,0},{48,16},{1,33},{17,49},{33,1},{49,17},{2,34}... | collective-permute-start | bytes 258056 | tf_op jit(solution)/shard_map/ppermute | solution.py:403
  9.4 4.5 %collective-permute-start.3 = (f16[336,128]{1,0:T(8,128)(2,1)S(1)}, f16[336,128]{1,0:T(8,128)(2,1)S(1)}, u32[]{:S(2)}, u32[]{:S(2)}) collective-permute-start(f16[336,128]{1,0:T(8,128)(2,1)S(1)} %get-tuple-element.20), channel_id=1, source_target_pairs={{0,48},{16,0},{32,16},{48,32},{1,49},{17,1},{33,17},{49,33},{2,50}... | collective-permute-start | bytes 258056 | tf_op jit(solution)/shard_map/ppermute | solution.py:403
  14.2 6.1 %collective-permute-start.4 = (f16[336,128]{1,0:T(8,128)(2,1)S(1)}, f16[336,128]{1,0:T(8,128)(2,1)S(1)}, u32[]{:S(2)}, u32[]{:S(2)}) collective-permute-start(f16[336,128]{1,0:T(8,128)(2,1)S(1)} %select_convert_fusion.1), channel_id=1, source_target_pairs={{0,64},{64,0},{1,65},{65,1},{2,66},{66,2},{3,67},{67,3},{4,68},{68... | collective-permute-start | bytes 258056 | tf_op jit(solution)/shard_map/ppermute | solution.py:403
  20.6 4.8 %collective-permute-start.7 = (f16[336,128]{1,0:T(8,128)(2,1)S(1)}, f16[336,128]{1,0:T(8,128)(2,1)S(1)}, u32[]{:S(2)}, u32[]{:S(2)}) collective-permute-start(f16[336,128]{1,0:T(8,128)(2,1)S(1)} %select_convert_fusion), channel_id=1, source_target_pairs={{0,48},{16,0},{32,16},{48,32},{1,49},{17,1},{33,17},{49,33},{2,50}... | collective-permute-start | bytes 258056 | tf_op jit(solution)/shard_map/ppermute | solution.py:403
  23.3 6.0 %collective-permute-start.6 = (f16[336,128]{1,0:T(8,128)(2,1)S(1)}, f16[336,128]{1,0:T(8,128)(2,1)S(1)}, u32[]{:S(2)}, u32[]{:S(2)}) collective-permute-start(f16[336,128]{1,0:T(8,128)(2,1)S(1)} %select_convert_fusion), channel_id=1, source_target_pairs={{0,32},{16,48},{32,0},{48,16},{1,33},{17,49},{33,1},{49,17},{2,34}... | collective-permute-start | bytes 258056 | tf_op jit(solution)/shard_map/ppermute | solution.py:403
  24.0 6.2 %collective-permute-start.5 = (f16[336,128]{1,0:T(8,128)(2,1)S(1)}, f16[336,128]{1,0:T(8,128)(2,1)S(1)}, u32[]{:S(2)}, u32[]{:S(2)}) collective-permute-start(f16[336,128]{1,0:T(8,128)(2,1)S(1)} %select_convert_fusion), channel_id=1, source_target_pairs={{0,16},{16,32},{32,48},{48,0},{1,17},{17,33},{33,49},{49,1},{2,18}... | collective-permute-start | bytes 258056 | tf_op jit(solution)/shard_map/ppermute | solution.py:403
  40.6 7.9 %collective-permute-start.8 = (bf16[512,512]{1,0:T(8,128)(2,1)S(1)}, bf16[512,512]{1,0:T(8,128)(2,1)S(1)}, u32[]{:S(2)}, u32[]{:S(2)}) collective-permute-start(bf16[512,512]{1,0:T(8,128)(2,1)S(1)} %rotation.1.rot_ref.refs_2_), channel_id=1, source_target_pairs={{0,8},{8,0},{1,9},{9,1},{2,10},{10,2},{3,11},{11,3},{4,12},{12,4},... | collective-permute-start | bytes 1572872 | tf_op jit(solution)/shard_map/ppermute | solution.py:403
  42.7 15.2 %collective-permute-start.10 = (bf16[1024,256]{1,0:T(8,128)(2,1)}, bf16[1024,256]{1,0:T(8,128)(2,1)}, u32[]{:S(2)}, u32[]{:S(2)}) collective-permute-start(bf16[1024,256]{1,0:T(8,128)(2,1)} %edge.3), channel_id=1, source_target_pairs={{1,0},{2,1},{3,2},{4,3},{5,4},{6,5},{7,6},{8,9},{9,10},{10,11},{11... | collective-permute-start | bytes 1572872 | tf_op jit(solution)/shard_map/ppermute | solution.py:413
  50.3 13.5 %collective-permute-start.9 = (bf16[1024,256]{1,0:T(8,128)(2,1)}, bf16[1024,256]{1,0:T(8,128)(2,1)}, u32[]{:S(2)}, u32[]{:S(2)}) collective-permute-start(bf16[1024,256]{1,0:T(8,128)(2,1)} %edge.2), channel_id=1, source_target_pairs={{0,1},{1,2},{2,3},{3,4},{4,5},{5,6},{6,7},{9,8},{10,9},{11,10},{12... | collective-permute-start | bytes 1572872 | tf_op jit(solution)/shard_map/ppermute | solution.py:413
